TPU v7x, 512 devices: a whole 4x8x8 slice. The times are simulated.
512 devices in a mesh: patch: 64 (over z, y), field: 8 (over x, core).
Axes of the slice: x: 4, y: 8, z: 8, core: 2. Of those that a mesh axis runs over, the one named last changes fastest.
Arguments:
- pressure_start: float32 [512, 32, 1024], P('patch', 'field'), may hold values from -6 to 6
- divergence: float32 [512, 32, 1024], P('patch', 'field'), may hold values from -6 to 6
- neighbors: int32 [512, 6], P('patch'), may hold values from -1 to 511, as said below
- advect_slot: int32 [512], P('patch'), may hold values from 0 to 63, as said below
- point_cell: int32 [8192], replicated, may hold values from 0 to 16777215
- point_force: float32 [8192], P(('patch', 'field')), may hold values from -24 to 24
Outputs:
- remapped: bfloat16 [4096, 3, 32, 1024], P('patch', None, 'field')
Inputs may be any that keep to these rules, and one draw needn't show every extreme that they name: `neighbors`: the low x neighbour of a patch held by index i of patch is held by index i - 1 and the high x neighbour by index i + 1, -1 where the domain ends in x; the y and z neighbours are held by the same index of patch as the patch. `advect_slot`: the 8 patches of one index of patch all have different entries; one owner, the same for every source, receives one patch from every index of patch.
All inputs are finite; a program needn't handle non-finite values.
Results may differ from a plain program's by a relative error of at most 0.0045.
Values may be sent and summed in bfloat16 or wider, within the bound.
A program may use at most 64 MiB of HBM per device.

v0:
```python
import jax
import jax.numpy as jnp
from jax import lax
from jax.sharding import PartitionSpec as P

SIDE = 32
SWEEPS = 6


relaxation = 1.0 / 9.0


def extended(value, sides, width):
    for axis, dim in sides:
        size, length = (lax.axis_size(axis), value.shape[dim])
        up = [(i, (i + 1) % size) for i in range(size - 1)]
        down = [(j, i) for i, j in up]
        last = lax.slice_in_dim(value, length - width, length, axis=dim)
        first = lax.slice_in_dim(value, 0, width, axis=dim)
        before = lax.ppermute(last, axis, up)
        after = lax.ppermute(first, axis, down)
        value = jnp.concatenate([before, value, after], axis=dim)
    return value


def side_faces(pressure, link_table):
    plane_area = pressure.shape[-1]
    south_face = pressure[:, :, plane_area - SIDE :][link_table[:, 2]]
    north_face = pressure[:, :, :SIDE][link_table[:, 3]]
    below_face = pressure[:, :, SIDE - 1 :: SIDE][link_table[:, 4]]
    above_face = pressure[:, :, 0::SIDE][link_table[:, 5]]
    return (south_face, north_face, below_face, above_face)


def stencil_values(pressure, west_plane, east_plane, side_rows):
    plane_area = pressure.shape[-1]
    cell_index = jnp.arange(plane_area, dtype=jnp.int32)
    y_index = cell_index // SIDE
    z_index = cell_index % SIDE
    south_face, north_face, below_face, above_face = side_rows
    to_west = jnp.concatenate([west_plane[:, None], pressure[:, :-1]], axis=1)
    to_east = jnp.concatenate([pressure[:, 1:], east_plane[:, None]], axis=1)
    to_south = jnp.where(
        y_index == 0, jnp.tile(south_face, (1, 1, SIDE)), jnp.roll(pressure, SIDE, axis=-1)
    )
    to_north = jnp.where(
        y_index == SIDE - 1, jnp.tile(north_face, (1, 1, SIDE)), jnp.roll(pressure, -SIDE, axis=-1)
    )
    to_below = jnp.where(
        z_index == 0, jnp.repeat(below_face, SIDE, axis=-1), jnp.roll(pressure, 1, axis=-1)
    )
    to_above = jnp.where(
        z_index == SIDE - 1, jnp.repeat(above_face, SIDE, axis=-1), jnp.roll(pressure, -1, axis=-1)
    )
    return (to_west, to_east, to_south, to_north, to_below, to_above)


def sweep(pressure, source, values):
    to_west, to_east, to_south, to_north, to_below, to_above = values
    neighbor_sum = to_west + to_east + to_south + to_north + to_below + to_above
    return pressure + relaxation * (source - (6.0 * pressure - neighbor_sum))


def gradient(values):
    to_west, to_east, to_south, to_north, to_below, to_above = values
    stacked = jnp.stack(
        [0.5 * (to_east - to_west), 0.5 * (to_north - to_south), 0.5 * (to_above - to_below)],
        axis=1,
    )
    return stacked.astype(jnp.bfloat16)


def on_device(pressure_start, divergence, neighbors, advect_slot, point_cell, point_force):
    patch_count = pressure_start.shape[0]
    slab_width = pressure_start.shape[1]
    plane_area = pressure_start.shape[2]
    patch_row = lax.axis_index("patch")
    field_row = lax.axis_index("field")
    field_count = lax.axis_size("field")
    owners = lax.axis_size("patch")
    first_patch = patch_row * patch_count
    local_links = neighbors - first_patch
    lower_index = jnp.clip(neighbors[:, 0] - (first_patch - patch_count), 0, patch_count - 1)
    upper_index = jnp.clip(neighbors[:, 1] - (first_patch + patch_count), 0, patch_count - 1)
    lower_valid = (neighbors[:, 0] >= 0)[:, None]
    upper_valid = (neighbors[:, 1] >= 0)[:, None]
    forces = lax.all_gather(point_force, ("patch", "field"), axis=0, tiled=True)
    volume = SIDE * SIDE * SIDE
    patch_of = point_cell // volume
    remainder = point_cell % volume
    plane_of = remainder // plane_area
    in_plane = remainder % plane_area
    local_patch = patch_of - first_patch
    local_plane = plane_of - field_row * slab_width
    inside = (
        (local_patch >= 0)
        & (local_patch < patch_count)
        & (local_plane >= 0)
        & (local_plane < slab_width)
    )
    target = jnp.where(
        inside,
        (local_patch * slab_width + local_plane) * plane_area + in_plane,
        patch_count * slab_width * plane_area,
    )
    source = divergence.reshape(-1).at[target].add(forces, mode="drop").reshape(divergence.shape)

    def ghost_planes(pressure):
        padded = extended(pressure.astype(jnp.bfloat16), ((("patch", "field"), 1),), 1).astype(
            pressure.dtype
        )
        lower_plane = padded[:, 0]
        upper_plane = padded[:, -1]
        west_plane = jnp.where(
            field_row == 0, jnp.where(lower_valid, lower_plane[lower_index], 0.0), lower_plane
        )
        east_plane = jnp.where(
            field_row == field_count - 1,
            jnp.where(upper_valid, upper_plane[upper_index], 0.0),
            upper_plane,
        )
        return (west_plane, east_plane)

    pressure = pressure_start
    for sweep_step in range(SWEEPS):
        west_plane, east_plane = ghost_planes(pressure)
        values = stencil_values(pressure, west_plane, east_plane, side_faces(pressure, local_links))
        pressure = sweep(pressure, source, values)
    west_plane, east_plane = ghost_planes(pressure)
    side_rows = side_faces(pressure, local_links)
    capacity = (2 * patch_count + owners - 1) // owners
    send_slots = owners * capacity
    gradients = gradient(stencil_values(pressure, west_plane, east_plane, side_rows))
    outgoing = (
        jnp.zeros((send_slots,) + gradients.shape[1:], jnp.bfloat16).at[advect_slot].set(gradients)
    )
    return lax.all_to_all(outgoing, "patch", split_axis=0, concat_axis=0, tiled=True)


def solution(mesh):
    in_specs = (
        P("patch", "field", None),
        P("patch", "field", None),
        P("patch", None),
        P("patch"),
        P(),
        P(("patch", "field")),
    )
    out_specs = P("patch", None, "field", None)
    return jax.shard_map(
        on_device, mesh=mesh, in_specs=in_specs, out_specs=out_specs, check_vma=False
    )
```

profile of v0, /device:TPU:7, one launch (start us, length us, event | category | flops | bytes accessed | tf_op | source)
XLA Modules:
  0.0 314.7 jit_solution(1966946139069522092)
XLA Ops:
  0.0 1.1 copy.119
  1.1 3.7 %collective-permute-start = (bf16[8,1,1024]{2,0,1:T(8,128)(2,1)S(1)}, bf16[8,1,1024]{2,0,1:T(8,128)(2,1)S(1)}, u32[]{:S(2)}, u32[]{:S(2)}) collective-permute-start(bf16[8,1,1024]{2,0,1:T(8,128)(2,1)S(1)} %get-tuple-element.151), channel_id=1, source_target_pairs={{0,1},{1,2},{2,3},{3,4},{4,5},{5,6},{6,7},{7,8},{8,9},{9,10},{10,1... | collective-permute-start | bytes 49160 | tf_op jit(solution)/shard_map/ppermute | solution.py:20
  4.8 1.9 collective-permute-start.1
  6.8 1.0 compare_reduce_fusion
  10.1 1.1 fusion.119
  11.2 1.1 fusion.122
  16.2 104.5 %all-reduce = f32[8192]{0:T(1024)S(1)} all-reduce(f32[8192]{0:T(1024)S(1)} %dynamic-update-slice), channel_id=1, replica_groups=mesh['patch'=64,'field'=8] {'patch','field'}, use_global_device_ids=true, to_apply=%add | all-reduce | flops 8192 | bytes 65536
  120.7 44.3 %scatter_fusion = f32[32768]{0:T(1024)S(1)} fusion(f32[32768]{0:T(1024)S(1)} %bitcast.223, s32[8192]{0:T(1024)S(1)} %compare_select_fusion, f32[8192]{0:T(1024)S(1)} %all-reduce), kind=kCustom, calls=%fused_computation.42 | custom fusion | flops 8192 | bytes 131072 | tf_op jit(solution)/shard_map/scatter-add | solution.py:106
  168.8 3.4 %collective-permute-start.2 = (bf16[8,1,1024]{2,0,1:T(8,128)(2,1)S(1)}, bf16[8,1,1024]{2,0,1:T(8,128)(2,1)S(1)}, u32[]{:S(2)}, u32[]{:S(2)}) collective-permute-start(bf16[8,1,1024]{2,0,1:T(8,128)(2,1)S(1)} %get-tuple-element.149), channel_id=1, source_target_pairs={{0,1},{1,2},{2,3},{3,4},{4,5},{5,6},{6,7},{7,8},{8,9},{9,10},{10,1... | collective-permute-start | bytes 49160 | tf_op jit(solution)/shard_map/ppermute | solution.py:20
  172.2 1.9 collective-permute-start.3
  181.2 4.9 %collective-permute-start.4 = (bf16[8,1,1024]{2,0,1:T(8,128)(2,1)S(1)}, bf16[8,1,1024]{2,0,1:T(8,128)(2,1)S(1)}, u32[]{:S(2)}, u32[]{:S(2)}) collective-permute-start(bf16[8,1,1024]{2,0,1:T(8,128)(2,1)S(1)} %get-tuple-element.147), channel_id=1, source_target_pairs={{0,1},{1,2},{2,3},{3,4},{4,5},{5,6},{6,7},{7,8},{8,9},{9,10},{10,1... | collective-permute-start | bytes 49160 | tf_op jit(solution)/shard_map/ppermute | solution.py:20
  186.1 1.9 collective-permute-start.5
  192.4 0.9 collective-permute-done.5
  195.1 4.9 %collective-permute-start.6 = (bf16[8,1,1024]{2,0,1:T(8,128)(2,1)S(1)}, bf16[8,1,1024]{2,0,1:T(8,128)(2,1)S(1)}, u32[]{:S(2)}, u32[]{:S(2)}) collective-permute-start(bf16[8,1,1024]{2,0,1:T(8,128)(2,1)S(1)} %get-tuple-element.145), channel_id=1, source_target_pairs={{0,1},{1,2},{2,3},{3,4},{4,5},{5,6},{6,7},{7,8},{8,9},{9,10},{10,1... | collective-permute-start | bytes 49160 | tf_op jit(solution)/shard_map/ppermute | solution.py:20
  200.0 2.1 collective-permute-start.7
  209.0 5.1 %collective-permute-start.8 = (bf16[8,1,1024]{2,0,1:T(8,128)(2,1)S(1)}, bf16[8,1,1024]{2,0,1:T(8,128)(2,1)S(1)}, u32[]{:S(2)}, u32[]{:S(2)}) collective-permute-start(bf16[8,1,1024]{2,0,1:T(8,128)(2,1)S(1)} %get-tuple-element.143), channel_id=1, source_target_pairs={{0,1},{1,2},{2,3},{3,4},{4,5},{5,6},{6,7},{7,8},{8,9},{9,10},{10,1... | collective-permute-start | bytes 49160 | tf_op jit(solution)/shard_map/ppermute | solution.py:20
  214.1 1.9 collective-permute-start.9
  223.1 4.9 %collective-permute-start.10 = (bf16[8,1,1024]{2,0,1:T(8,128)(2,1)S(1)}, bf16[8,1,1024]{2,0,1:T(8,128)(2,1)S(1)}, u32[]{:S(2)}, u32[]{:S(2)}) collective-permute-start(bf16[8,1,1024]{2,0,1:T(8,128)(2,1)S(1)} %get-tuple-element.141), channel_id=1, source_target_pairs={{0,1},{1,2},{2,3},{3,4},{4,5},{5,6},{6,7},{7,8},{8,9},{9,10},{10,1... | collective-permute-start | bytes 49160 | tf_op jit(solution)/shard_map/ppermute | solution.py:20
  228.0 1.9 collective-permute-start.11
  238.6 4.9 %collective-permute-start.12 = (bf16[8,1,1024]{2,0,1:T(8,128)(2,1)S(1)}, bf16[8,1,1024]{2,0,1:T(8,128)(2,1)S(1)}, u32[]{:S(2)}, u32[]{:S(2)}) collective-permute-start(bf16[8,1,1024]{2,0,1:T(8,128)(2,1)S(1)} %get-tuple-element.139), channel_id=1, source_target_pairs={{0,1},{1,2},{2,3},{3,4},{4,5},{5,6},{6,7},{7,8},{8,9},{9,10},{10,1... | collective-permute-start | bytes 49160 | tf_op jit(solution)/shard_map/ppermute | solution.py:20
  243.5 1.9 collective-permute-start.13
  248.4 2.3 collective-permute-done.13
  253.4 60.1 %all_to_all.5 = bf16[64,3,4,1024]{3,2,1,0:T(4,128)(2,1)S(1)} all-to-all(bf16[64,3,4,1024]{3,2,1,0:T(4,128)(2,1)S(1)} %scatter_fusion.1), channel_id=1, replica_groups=mesh['patch'=64,'field'=8] {'patch'}, dimensions={0} | all-to-all | bytes 3145728 | tf_op jit(solution)/shard_map/all_to_all | solution.py:137
  313.5 1.1 copy.131
  (288 shorter events, 50.2 us)
Async XLA Ops:
  0.0 12.3 %copy-start = (f32[8,4,1024]{2,1,0:T(4,128)S(1)}, f32[8,4,1024]{2,1,0:T(4,128)}, u32[]{:S(2)}) copy-start(f32[8,4,1024]{2,1,0:T(4,128)} %param.6) | copy-start | bytes 393220
  0.0 12.4 %copy-start.2 = (s32[8,6]{1,0:T(8,128)S(1)}, s32[8,6]{1,0:T(8,128)}, u32[]{:S(2)}) copy-start(s32[8,6]{1,0:T(8,128)} %param.8) | copy-start | bytes 580
  0.0 12.4 %copy-start.4 = (s32[8]{0:T(128)S(1)}, s32[8]{0:T(128)}, u32[]{:S(2)}) copy-start(s32[8]{0:T(128)} %param.9) | copy-start | bytes 100
  0.0 12.8 %copy-start.3 = (s32[8192]{0:T(1024)S(1)}, s32[8192]{0:T(1024)}, u32[]{:S(2)}) copy-start(s32[8192]{0:T(1024)} %param.10) | copy-start | bytes 98308
  0.0 15.9 %copy-start.1 = (f32[8,4,1024]{2,1,0:T(4,128)S(1)}, f32[8,4,1024]{2,1,0:T(4,128)}, u32[]{:S(2)}) copy-start(f32[8,4,1024]{2,1,0:T(4,128)} %param.7) | copy-start | bytes 393220
  0.0 15.9 %copy-start.5 = (f32[16]{0:T(128)S(1)}, f32[16]{0:T(128)}, u32[]{:S(2)}) copy-start(f32[16]{0:T(128)} %param.11) | copy-start | bytes 196
  1.1 165.9 %collective-permute-start = (bf16[8,1,1024]{2,0,1:T(8,128)(2,1)S(1)}, bf16[8,1,1024]{2,0,1:T(8,128)(2,1)S(1)}, u32[]{:S(2)}, u32[]{:S(2)}) collective-permute-start(bf16[8,1,1024]{2,0,1:T(8,128)(2,1)S(1)} %get-tuple-element.151), channel_id=1, source_target_pairs={{0,1},{1,2},{2,3},{3,4},{4,5},{5,6},{6,7},{7,8},{8,9},{9,10},{10,1... | collective-permute-start | bytes 49160 | tf_op jit(solution)/shard_map/ppermute | solution.py:20
  4.8 162.2 %collective-permute-start.1 = (bf16[8,1,1024]{2,0,1:T(8,128)(2,1)S(1)}, bf16[8,1,1024]{2,0,1:T(8,128)(2,1)S(1)}, u32[]{:S(2)}, u32[]{:S(2)}) collective-permute-start(bf16[8,1,1024]{2,0,1:T(8,128)(2,1)S(1)} %get-tuple-element.152), channel_id=1, source_target_pairs={{1,0},{2,1},{3,2},{4,3},{5,4},{6,5},{7,6},{8,7},{9,8},{10,9},{11,1... | collective-permute-start | bytes 49160 | tf_op jit(solution)/shard_map/ppermute | solution.py:21
  168.8 9.7 %collective-permute-start.2 = (bf16[8,1,1024]{2,0,1:T(8,128)(2,1)S(1)}, bf16[8,1,1024]{2,0,1:T(8,128)(2,1)S(1)}, u32[]{:S(2)}, u32[]{:S(2)}) collective-permute-start(bf16[8,1,1024]{2,0,1:T(8,128)(2,1)S(1)} %get-tuple-element.149), channel_id=1, source_target_pairs={{0,1},{1,2},{2,3},{3,4},{4,5},{5,6},{6,7},{7,8},{8,9},{9,10},{10,1... | collective-permute-start | bytes 49160 | tf_op jit(solution)/shard_map/ppermute | solution.py:20
  172.2 7.2 %collective-permute-start.3 = (bf16[8,1,1024]{2,0,1:T(8,128)(2,1)S(1)}, bf16[8,1,1024]{2,0,1:T(8,128)(2,1)S(1)}, u32[]{:S(2)}, u32[]{:S(2)}) collective-permute-start(bf16[8,1,1024]{2,0,1:T(8,128)(2,1)S(1)} %get-tuple-element.150), channel_id=1, source_target_pairs={{1,0},{2,1},{3,2},{4,3},{5,4},{6,5},{7,6},{8,7},{9,8},{10,9},{11,1... | collective-permute-start | bytes 49160 | tf_op jit(solution)/shard_map/ppermute | solution.py:21
  181.2 11.2 %collective-permute-start.4 = (bf16[8,1,1024]{2,0,1:T(8,128)(2,1)S(1)}, bf16[8,1,1024]{2,0,1:T(8,128)(2,1)S(1)}, u32[]{:S(2)}, u32[]{:S(2)}) collective-permute-start(bf16[8,1,1024]{2,0,1:T(8,128)(2,1)S(1)} %get-tuple-element.147), channel_id=1, source_target_pairs={{0,1},{1,2},{2,3},{3,4},{4,5},{5,6},{6,7},{7,8},{8,9},{9,10},{10,1... | collective-permute-start | bytes 49160 | tf_op jit(solution)/shard_map/ppermute | solution.py:20
  186.1 7.2 %collective-permute-start.5 = (bf16[8,1,1024]{2,0,1:T(8,128)(2,1)S(1)}, bf16[8,1,1024]{2,0,1:T(8,128)(2,1)S(1)}, u32[]{:S(2)}, u32[]{:S(2)}) collective-permute-start(bf16[8,1,1024]{2,0,1:T(8,128)(2,1)S(1)} %get-tuple-element.148), channel_id=1, source_target_pairs={{1,0},{2,1},{3,2},{4,3},{5,4},{6,5},{7,6},{8,7},{9,8},{10,9},{11,1... | collective-permute-start | bytes 49160 | tf_op jit(solution)/shard_map/ppermute | solution.py:21
  195.1 11.3 %collective-permute-start.6 = (bf16[8,1,1024]{2,0,1:T(8,128)(2,1)S(1)}, bf16[8,1,1024]{2,0,1:T(8,128)(2,1)S(1)}, u32[]{:S(2)}, u32[]{:S(2)}) collective-permute-start(bf16[8,1,1024]{2,0,1:T(8,128)(2,1)S(1)} %get-tuple-element.145), channel_id=1, source_target_pairs={{0,1},{1,2},{2,3},{3,4},{4,5},{5,6},{6,7},{7,8},{8,9},{9,10},{10,1... | collective-permute-start | bytes 49160 | tf_op jit(solution)/shard_map/ppermute | solution.py:20
  200.0 7.2 %collective-permute-start.7 = (bf16[8,1,1024]{2,0,1:T(8,128)(2,1)S(1)}, bf16[8,1,1024]{2,0,1:T(8,128)(2,1)S(1)}, u32[]{:S(2)}, u32[]{:S(2)}) collective-permute-start(bf16[8,1,1024]{2,0,1:T(8,128)(2,1)S(1)} %get-tuple-element.146), channel_id=1, source_target_pairs={{1,0},{2,1},{3,2},{4,3},{5,4},{6,5},{7,6},{8,7},{9,8},{10,9},{11,1... | collective-permute-start | bytes 49160 | tf_op jit(solution)/shard_map/ppermute | solution.py:21
  209.0 11.3 %collective-permute-start.8 = (bf16[8,1,1024]{2,0,1:T(8,128)(2,1)S(1)}, bf16[8,1,1024]{2,0,1:T(8,128)(2,1)S(1)}, u32[]{:S(2)}, u32[]{:S(2)}) collective-permute-start(bf16[8,1,1024]{2,0,1:T(8,128)(2,1)S(1)} %get-tuple-element.143), channel_id=1, source_target_pairs={{0,1},{1,2},{2,3},{3,4},{4,5},{5,6},{6,7},{7,8},{8,9},{9,10},{10,1... | collective-permute-start | bytes 49160 | tf_op jit(solution)/shard_map/ppermute | solution.py:20
  214.1 7.2 %collective-permute-start.9 = (bf16[8,1,1024]{2,0,1:T(8,128)(2,1)S(1)}, bf16[8,1,1024]{2,0,1:T(8,128)(2,1)S(1)}, u32[]{:S(2)}, u32[]{:S(2)}) collective-permute-start(bf16[8,1,1024]{2,0,1:T(8,128)(2,1)S(1)} %get-tuple-element.144), channel_id=1, source_target_pairs={{1,0},{2,1},{3,2},{4,3},{5,4},{6,5},{7,6},{8,7},{9,8},{10,9},{11,1... | collective-permute-start | bytes 49160 | tf_op jit(solution)/shard_map/ppermute | solution.py:21
  223.1 11.2 %collective-permute-start.10 = (bf16[8,1,1024]{2,0,1:T(8,128)(2,1)S(1)}, bf16[8,1,1024]{2,0,1:T(8,128)(2,1)S(1)}, u32[]{:S(2)}, u32[]{:S(2)}) collective-permute-start(bf16[8,1,1024]{2,0,1:T(8,128)(2,1)S(1)} %get-tuple-element.141), channel_id=1, source_target_pairs={{0,1},{1,2},{2,3},{3,4},{4,5},{5,6},{6,7},{7,8},{8,9},{9,10},{10,1... | collective-permute-start | bytes 49160 | tf_op jit(solution)/shard_map/ppermute | solution.py:20
  228.0 7.2 %collective-permute-start.11 = (bf16[8,1,1024]{2,0,1:T(8,128)(2,1)S(1)}, bf16[8,1,1024]{2,0,1:T(8,128)(2,1)S(1)}, u32[]{:S(2)}, u32[]{:S(2)}) collective-permute-start(bf16[8,1,1024]{2,0,1:T(8,128)(2,1)S(1)} %get-tuple-element.142), channel_id=1, source_target_pairs={{1,0},{2,1},{3,2},{4,3},{5,4},{6,5},{7,6},{8,7},{9,8},{10,9},{11,1... | collective-permute-start | bytes 49160 | tf_op jit(solution)/shard_map/ppermute | solution.py:21
  238.6 9.7 %collective-permute-start.12 = (bf16[8,1,1024]{2,0,1:T(8,128)(2,1)S(1)}, bf16[8,1,1024]{2,0,1:T(8,128)(2,1)S(1)}, u32[]{:S(2)}, u32[]{:S(2)}) collective-permute-start(bf16[8,1,1024]{2,0,1:T(8,128)(2,1)S(1)} %get-tuple-element.139), channel_id=1, source_target_pairs={{0,1},{1,2},{2,3},{3,4},{4,5},{5,6},{6,7},{7,8},{8,9},{9,10},{10,1... | collective-permute-start | bytes 49160 | tf_op jit(solution)/shard_map/ppermute | solution.py:20
  243.5 7.2 %collective-permute-start.13 = (bf16[8,1,1024]{2,0,1:T(8,128)(2,1)S(1)}, bf16[8,1,1024]{2,0,1:T(8,128)(2,1)S(1)}, u32[]{:S(2)}, u32[]{:S(2)}) collective-permute-start(bf16[8,1,1024]{2,0,1:T(8,128)(2,1)S(1)} %get-tuple-element.140), channel_id=1, source_target_pairs={{1,0},{2,1},{3,2},{4,3},{5,4},{6,5},{7,6},{8,7},{9,8},{10,9},{11,1... | collective-permute-start | bytes 49160 | tf_op jit(solution)/shard_map/ppermute | solution.py:21
where the time goes:
time: 315 us
  blocking collectives  165 us (52%)
  other arithmetic  49.1 us (16%)
  local copies, waits for them, and re-layouts  47.3 us (15%)
  starting transfers between devices  45.3 us (14%)
  waiting for transfers between devices  6.58 us (2%)
    unnamed x1, blocking collectives  104 us
    all_to_all x1, blocking collectives, on_device(): lax.all_to_all(outgoing, 'patch', split_axis=0, concat_axis=0, tiled=True)  60.1 us
    scatter-add x1, other arithmetic, on_device(): divergence.reshape(-1).at[target].add(forces, mode='drop')  44.3 us
    ppermute x7, starting transfers between devices, extended(): before = lax.ppermute(last, axis, up)  31.7 us
    ppermute x7, starting transfers between devices, extended(): after = lax.ppermute(first, axis, down)  13.6 us
    ppermute x7, waiting for transfers between devices, extended(): after = lax.ppermute(first, axis, down)  6.57 us
  transfers between devices with their start and end apart: 14, of which 6 were waited for; matrix products, arithmetic and copies ran while one was open for 25% of the time, Pallas kernels for 0%

commit v1 on v0

v1 whole, which is shorter than its diff:
```python
import functools
import math

import jax
import jax.numpy as jnp
from jax import lax
from jax.experimental import pallas as pl
from jax.experimental.pallas import tpu as pltpu
from jax.sharding import PartitionSpec as P

SIDE = 32
SWEEPS = 6
PPD = 8
PLANES = 4
AREA = SIDE * SIDE
CHUNKS = AREA // 128
SLABS = 5
LANES = 128
REGION = 16
ROWS_HOT = REGION * PPD * (AREA // 256)
MESH = pl.DeviceIdType.MESH

relaxation = 1.0 / 9.0


def lane_iota():
    return lax.broadcasted_iota(jnp.int32, (PPD, LANES), 1)


def by_patch(value, index):
    return jnp.take_along_axis(value, index, axis=0, mode="promise_in_bounds")


def by_lane(value, index):
    return jnp.take_along_axis(value, index, axis=1, mode="promise_in_bounds")


def side_values(center, idx_south, idx_north, idx_z):
    lane = lane_iota()
    z = lane % SIDE
    up = [pltpu.roll(c, SIDE, 1) for c in center]
    down = [pltpu.roll(c, LANES - SIDE, 1) for c in center]
    first = by_patch(up[CHUNKS - 1], idx_south)
    last = by_patch(down[0], idx_north)
    south, north, below, above, faces = [], [], [], [], []
    for v in range(CHUNKS):
        south.append(jnp.where(lane < SIDE, first if v == 0 else up[v - 1], up[v]))
        north.append(
            jnp.where(lane >= LANES - SIDE, last if v == CHUNKS - 1 else down[v + 1], down[v])
        )
        swapped = jnp.where(
            z == 0,
            pltpu.roll(center[v], LANES - (SIDE - 1), 1),
            pltpu.roll(center[v], SIDE - 1, 1),
        )
        face = by_patch(swapped, idx_z)
        faces.append(face)
        below.append(jnp.where(z == 0, face, pltpu.roll(center[v], 1, 1)))
        above.append(jnp.where(z == SIDE - 1, face, pltpu.roll(center[v], LANES - 1, 1)))
    return south, north, below, above, faces


def chunks_of(ref, k, row):
    return [ref[k, row, :, v * LANES : (v + 1) * LANES] for v in range(CHUNKS)]


def step_kernel(
    nz,
    ny,
    nf,
    inv_ref,
    p_ref,
    d_ref,
    tab_ref,
    frow_ref,
    pc_ref,
    out_ref,
    pa,
    pb,
    src,
    tabs,
    xbuf,
    ybuf,
    forces,
    hot_a,
    hot_b,
    scaled,
    acc,
    idx,
    packed,
    sbuf,
    load_sem,
    halo_send,
    halo_recv,
    x_send,
    x_recv,
    y_send,
    y_recv,
    z_send,
    z_recv,
    a_send,
    a_recv,
    own_sem,
):
    patch = lax.axis_index("patch")
    field = lax.axis_index("field")
    z_me = lax.div(patch, ny)
    y_me = lax.rem(patch, ny)
    total = nz * ny * nf
    line = patch * nf + field
    x_side = PLANES * nf

    def along_line(k):
        other = lax.rem(line + (k + total), total)
        return (lax.div(other, nf), lax.rem(other, nf))

    def along_x(k):
        return (patch, lax.rem(field + k, nf))

    def along_y(k):
        return (z_me * ny + lax.rem(y_me + k, ny), field)

    def along_z(k):
        return (lax.rem(z_me + k, nz) * ny + y_me, field)

    loads = []
    for x in range(PLANES):
        loads.append(
            pltpu.make_async_copy(p_ref.at[:, x, :], pa.at[2, x + 1], load_sem.at[0, x])
        )
        loads.append(pltpu.make_async_copy(d_ref.at[:, x, :], src.at[2, x], load_sem.at[1, x]))
    loads.append(pltpu.make_async_copy(tab_ref, tabs.at[2], load_sem.at[0, PLANES]))
    for copy in loads:
        copy.start()

    barrier = pltpu.get_barrier_semaphore()
    greeted = [along_x(k) for k in range(1, nf)]
    greeted += [along_y(k) for k in range(1, ny)]
    greeted += [along_z(k) for k in range(1, nz)]
    greeted += [along_line(k) for k in (1, -1, 2, -2)]
    for device in greeted:
        pl.semaphore_signal(barrier, inc=1, device_id=device, device_id_type=MESH)

    def build_hot(row, carry):
        zrow = lax.div(row, ny)
        yrow = lax.rem(row, ny)
        cell = pc_ref[pl.ds(row, 1), :]
        q = cell // (x_side * AREA)
        inside = cell % (x_side * AREA)
        plane = lax.div(q, PPD) * x_side + lax.div(inside, AREA)
        lp = lax.rem(q, PPD)
        cell_in_plane = lax.rem(inside, AREA)
        e = plane - (line * PLANES - 6)
        m = (lax.div(cell_in_plane, 256) * REGION + e) * PPD + lp
        m = jnp.where((e >= 0) & (e < REGION), m, -1)
        n = lax.rem(cell_in_plane, 256)
        lanes = pl.ds(pl.multiple_of(yrow * LANES, LANES), LANES)
        rows = lax.broadcasted_iota(jnp.int32, (ROWS_HOT, LANES), 0)
        hot_a[zrow, :, lanes] = jnp.where(rows == m, 1.0, 0.0).astype(jnp.bfloat16)
        columns = lax.broadcasted_iota(jnp.int32, (256, LANES), 0)
        hot_b[zrow, :, lanes] = jnp.where(columns == n, 1.0, 0.0).astype(jnp.bfloat16)
        return carry

    half = nz * ny // 2
    lax.fori_loop(0, half, build_hot, 0)
    for copy in loads:
        copy.wait()
    pl.semaphore_wait(barrier, len(greeted))

    def send(source, target, s_sem, r_sem, device):
        copy = pltpu.make_async_remote_copy(
            src_ref=source,
            dst_ref=target,
            send_sem=s_sem,
            recv_sem=r_sem,
            device_id=device,
            device_id_type=MESH,
        )
        copy.start()
        return copy

    x_copies = [
        send(frow_ref, xbuf.at[field], x_send.at[k - 1], x_recv.at[k - 1], along_x(k))
        for k in range(1, nf)
    ]
    halo = []
    for i, (k, lo, hi, dlo, dhi) in enumerate(
        ((1, 0, 4, 0, 4), (-1, 0, 4, 0, 4), (2, 1, 4, 2, 4), (-2, 0, 3, 0, 2))
    ):
        there = along_line(k)
        slot = 2 - k
        halo.append(
            send(
                pa.at[2, lo + 1 : hi + 1],
                pa.at[slot, lo + 1 : hi + 1],
                halo_send.at[0, i],
                halo_recv.at[0, i],
                there,
            )
        )
        halo.append(
            send(
                src.at[2, dlo:dhi],
                src.at[slot, dlo:dhi],
                halo_send.at[1, i],
                halo_recv.at[1, i],
                there,
            )
        )
        halo.append(
            send(tabs.at[2], tabs.at[slot], halo_send.at[2, i], halo_recv.at[2, i], there)
        )

    lax.fori_loop(half, nz * ny, build_hot, 0)

    for copy in x_copies:
        copy.wait_recv()
    row = frow_ref[...]
    for k in range(1, nf):
        row = row + xbuf[lax.rem(field + k, nf)]
    ybuf[y_me] = row
    y_copies = [
        send(ybuf.at[y_me], ybuf.at[y_me], y_send.at[k - 1], y_recv.at[k - 1], along_y(k))
        for k in range(1, ny)
    ]
    acc[...] = jnp.zeros_like(acc)
    for copy in y_copies:
        copy.wait_recv()
    z_copies = [
        send(ybuf, forces.at[z_me], z_send.at[k - 1], z_recv.at[k - 1], along_z(k))
        for k in range(1, nz)
    ]
    forces[z_me] = ybuf[...]

    def add_points(zrow):
        for part in range(2):
            for yrow in range(ny):
                force = forces[zrow, yrow]
                high = force.astype(jnp.bfloat16)
                if part == 1:
                    high = (force - high.astype(jnp.float32)).astype(jnp.bfloat16)
                wide = jnp.broadcast_to(high.astype(jnp.float32), (16, LANES)).astype(jnp.bfloat16)
                for b in range(16):
                    scaled[b * 16 : (b + 1) * 16, yrow * LANES : (yrow + 1) * LANES] = (
                        hot_b[zrow, b * 16 : (b + 1) * 16, yrow * LANES : (yrow + 1) * LANES] * wide
                    )
            acc[...] += lax.dot_general(
                hot_a[zrow],
                scaled[...],
                (((1,), (1,)), ((), ())),
                preferred_element_type=jnp.float32,
            )

    add_points(z_me)

    for copy in halo:
        copy.wait_recv()
    zero_idx = jnp.zeros((PPD, LANES), jnp.int32)
    own_row = lax.broadcasted_iota(jnp.int32, (PPD, LANES), 0)
    z_lane = lane_iota() % SIDE
    for k in range(SLABS):
        table = tabs[k]
        columns = [zero_idx + table[:, c : c + 1] for c in range(6)]
        fk = lax.rem(field + (k - 2 + nf), nf)
        idx[k, 0] = jnp.where(fk == 0, columns[0], own_row)
        idx[k, 1] = jnp.where(fk == nf - 1, columns[1], own_row)
        idx[k, 2] = columns[2] & (PPD - 1)
        idx[k, 3] = columns[3] & (PPD - 1)
        idx[k, 4] = jnp.where(z_lane == 0, columns[4], columns[5]) & (PPD - 1)

    def fill_ghosts(ref, edges):
        for k in edges:
            west, east = idx[k, 0], idx[k - 1, 1]
            west_values = chunks_of(ref, k - 1, PLANES)
            east_values = chunks_of(ref, k, 1)
            for v in range(CHUNKS):
                lanes = slice(v * LANES, (v + 1) * LANES)
                ref[k, 0, :, lanes] = jnp.where(
                    west >= 0, by_patch(west_values[v], west & (PPD - 1)), 0.0
                )
                ref[k - 1, PLANES + 1, :, lanes] = jnp.where(
                    east >= 0, by_patch(east_values[v], east & (PPD - 1)), 0.0
                )

    def sweep(old, new, lo, hi):
        def body(g, carry):
            k = lax.div(g, PLANES)
            j = lax.rem(g, PLANES)
            west = chunks_of(old, k, j)
            center = chunks_of(old, k, j + 1)
            east = chunks_of(old, k, j + 2)
            south, north, below, above, _ = side_values(center, idx[k, 2], idx[k, 3], idx[k, 4])
            for v in range(CHUNKS):
                around = west[v] + east[v] + south[v] + north[v] + below[v] + above[v]
                source = src[k, j, :, v * LANES : (v + 1) * LANES]
                new[k, j + 1, :, v * LANES : (v + 1) * LANES] = center[v] + relaxation * (
                    source - (6.0 * center[v] - around)
                )
            return carry

        lax.fori_loop(lo, hi + 1, body, 0)

    fill_ghosts(pa, range(1, SLABS))
    for copy in halo:
        copy.wait_send()
    sweep(pa, pb, 2, 17)

    for k in range(1, nz):
        z_copies[k - 1].wait_recv()
        add_points(lax.rem(z_me + (nz - k), nz))

    for e in range(REGION):
        k, j = divmod(e + 2, PLANES)
        for part in range(AREA // 256):
            extra = acc[(part * REGION + e) * PPD : (part * REGION + e + 1) * PPD, :]
            lanes = slice(part * 256, (part + 1) * 256)
            src[k, j, :, lanes] += extra
            pb[k, j + 1, :, lanes] += relaxation * extra

    refs = (pa, pb)
    for t in range(2, SWEEPS + 1):
        old, new = refs[(t + 1) % 2], refs[t % 2]
        reach = SWEEPS - t
        fill_ghosts(old, range(1, SLABS) if reach >= 1 else (2, 3))
        sweep(old, new, 7 - reach, 12 + reach)
    final = refs[SWEEPS % 2]
    fill_ghosts(final, (2, 3))

    values = [chunks_of(final, 2, r) for r in range(PLANES + 2)]
    level = values[1][0]
    for r in range(1, PLANES + 1):
        for v in range(CHUNKS):
            if (r, v) != (1, 0):
                level = level + values[r][v]
    level = jnp.sum(level, axis=1, keepdims=True) * (1.0 / (PLANES * AREA))
    lane = lane_iota()
    group = lane // SIDE
    within = lane % SIDE
    chunk_of_lane = within // 4
    face_lane = (within % 4) * SIDE + jnp.where(group == 2, SIDE - 1, 0)
    for r in range(PLANES + 2):
        for v in range(CHUNKS):
            packed[:PPD, r, v, :] = values[r][v] - level
    for r in range(1, PLANES + 1):
        south, north, _, _, faces = side_values(values[r], idx[2, 2], idx[2, 3], idx[2, 4])
        row = jnp.where(group == 0, south[0], north[CHUNKS - 1])
        for v in range(CHUNKS):
            use = (chunk_of_lane == v) & ((group == 1) | (group == 2))
            row = jnp.where(use, by_lane(faces[v], face_lane), row)
        packed[:PPD, PLANES + 2, r - 1, :] = row - level
        packed[:PPD, PLANES + 2, PLANES + r - 1, :] = jnp.zeros_like(row)
    packed[PPD] = jnp.zeros_like(packed[PPD])

    def fill_slot(d, carry):
        sbuf[d] = packed[inv_ref[d]].astype(jnp.bfloat16)
        return carry

    lax.fori_loop(0, nz * ny, fill_slot, 0)

    def remap_copy(i):
        a, b = lax.div(i, ny), lax.rem(i, ny)
        dz = lax.rem(a + b, nz)
        there = lax.rem(z_me + dz, nz) * ny + lax.rem(y_me + b, ny)
        return pltpu.make_async_remote_copy(
            src_ref=sbuf.at[there],
            dst_ref=out_ref.at[patch],
            send_sem=a_send.at[i],
            recv_sem=a_recv.at[i],
            device_id=(there, field),
            device_id_type=MESH,
        )

    def start_copy(i, carry):
        remap_copy(i).start()
        return carry

    def wait_copy(i, carry):
        remap_copy(i).wait()
        return carry

    own = pltpu.make_async_copy(sbuf.at[patch], out_ref.at[patch], own_sem)
    own.start()
    lax.fori_loop(1, nz * ny, start_copy, 0)
    for copy in x_copies + y_copies + z_copies:
        copy.wait_send()
    own.wait()
    lax.fori_loop(1, nz * ny, wait_copy, 0)


def gradient_kernel(in_ref, out_ref, turn):
    lane = lane_iota()
    chunk = lax.broadcasted_iota(jnp.int32, (CHUNKS, LANES), 0)
    z = lane % SIDE
    face_lane = jnp.where(z == 0, SIDE, 2 * SIDE) + chunk * 4 + lane // SIDE
    low_corner = (chunk == 0) & (lane < SIDE)
    high_corner = (chunk == CHUNKS - 1) & (lane >= LANES - SIDE)

    def body(s, carry):
        rows = [in_ref[s, r].astype(jnp.float32) for r in range(PLANES + 3)]
        for x in range(PLANES):
            center = rows[x + 1]
            face = jnp.broadcast_to(rows[PLANES + 2][x : x + 1, :], (CHUNKS, LANES))
            face_z = by_lane(face, face_lane)
            up = pltpu.roll(center, SIDE, 1)
            down = pltpu.roll(center, LANES - SIDE, 1)
            south = jnp.where(lane < SIDE, pltpu.roll(up, 1, 0), up)
            south = jnp.where(low_corner, face, south)
            north = jnp.where(lane >= LANES - SIDE, pltpu.roll(down, CHUNKS - 1, 0), down)
            north = jnp.where(high_corner, face, north)
            below = jnp.where(z == 0, face_z, pltpu.roll(center, 1, 1))
            above = jnp.where(z == SIDE - 1, face_z, pltpu.roll(center, LANES - 1, 1))
            turn[0, x] = 0.5 * (rows[x + 2] - rows[x])
            turn[1, x] = 0.5 * (north - south)
            turn[2, x] = 0.5 * (above - below)
        for c in range(3):
            for v in range(CHUNKS):
                out_ref[s, c, :, v * LANES : (v + 1) * LANES] = turn[c, :, v, :].astype(jnp.bfloat16)
        return carry

    lax.fori_loop(0, in_ref.shape[0], body, 0)


def on_device(pressure_start, divergence, neighbors, advect_slot, point_cell, point_force):
    n_patch = lax.axis_size("patch")
    nf = lax.axis_size("field")
    ny = math.isqrt(n_patch)
    nz = n_patch // ny
    field = lax.axis_index("field")
    per_device = point_force.shape[0]
    lane = jnp.arange(LANES, dtype=jnp.int32)
    spread = jnp.tile(point_force, LANES // per_device)
    frow = jnp.where(lane // per_device == field, spread, 0.0).reshape(1, LANES)
    table = jnp.pad(neighbors, ((0, 0), (0, LANES - 6)))
    cells = point_cell.reshape(n_patch, -1)
    if cells.shape[1] < LANES:
        cells = jnp.pad(cells, ((0, 0), (0, LANES - cells.shape[1])), constant_values=-1)
    owner = jnp.arange(n_patch, dtype=jnp.int32)
    order = jnp.arange(PPD, dtype=jnp.int32)
    hit = advect_slot[:, None] == owner[None, :]
    inverse = PPD - jnp.sum(jnp.where(hit, PPD - order[:, None], 0), axis=0, dtype=jnp.int32)

    anywhere = pl.BlockSpec(memory_space=pl.ANY)
    vmem = pl.BlockSpec(memory_space=pltpu.VMEM)
    dma = pltpu.SemaphoreType.DMA
    slot = (PLANES + 3, CHUNKS, LANES)
    received = pl.pallas_call(
        functools.partial(step_kernel, nz, ny, nf),
        out_shape=jax.ShapeDtypeStruct((n_patch,) + slot, jnp.bfloat16),
        in_specs=[
            pl.BlockSpec(memory_space=pltpu.SMEM),
            anywhere,
            anywhere,
            anywhere,
            vmem,
            vmem,
        ],
        out_specs=anywhere,
        scratch_shapes=[
            pltpu.VMEM((SLABS, PLANES + 2, PPD, AREA), jnp.float32),
            pltpu.VMEM((SLABS, PLANES + 2, PPD, AREA), jnp.float32),
            pltpu.VMEM((SLABS, PLANES, PPD, AREA), jnp.float32),
            pltpu.VMEM((SLABS, PPD, LANES), jnp.int32),
            pltpu.VMEM((nf, 1, LANES), jnp.float32),
            pltpu.VMEM((ny, 1, LANES), jnp.float32),
            pltpu.VMEM((nz, ny, 1, LANES), jnp.float32),
            pltpu.VMEM((nz, ROWS_HOT, ny * LANES), jnp.bfloat16),
            pltpu.VMEM((nz, 256, ny * LANES), jnp.bfloat16),
            pltpu.VMEM((256, ny * LANES), jnp.bfloat16),
            pltpu.VMEM((ROWS_HOT, 256), jnp.float32),
            pltpu.VMEM((SLABS, 5, PPD, LANES), jnp.int32),
            pltpu.VMEM((PPD + 1,) + slot, jnp.float32),
            pltpu.VMEM((n_patch,) + slot, jnp.bfloat16),
            dma((2, PLANES + 1)),
            dma((3, 4)),
            dma((3, 4)),
            dma((nf - 1,)),
            dma((nf - 1,)),
            dma((ny - 1,)),
            dma((ny - 1,)),
            dma((nz - 1,)),
            dma((nz - 1,)),
            dma((n_patch,)),
            dma((n_patch,)),
            dma,
        ],
        compiler_params=pltpu.CompilerParams(
            collective_id=0, has_side_effects=True, vmem_limit_bytes=48 * 1024 * 1024
        ),
        name="step",
    )(inverse, pressure_start, divergence, table, frow, cells)

    block = 8 if n_patch % 8 == 0 else n_patch
    return pl.pallas_call(
        gradient_kernel,
        grid=(n_patch // block,),
        out_shape=jax.ShapeDtypeStruct((n_patch, 3, PLANES, AREA), jnp.bfloat16),
        in_specs=[pl.BlockSpec((block,) + slot, lambda i: (i, 0, 0, 0))],
        out_specs=pl.BlockSpec((block, 3, PLANES, AREA), lambda i: (i, 0, 0, 0)),
        scratch_shapes=[pltpu.VMEM((3, PLANES, CHUNKS, LANES), jnp.float32)],
        name="gradient",
    )(received)


def solution(mesh):
    in_specs = (
        P("patch", "field", None),
        P("patch", "field", None),
        P("patch", None),
        P("patch"),
        P(),
        P(("patch", "field")),
    )
    out_specs = P("patch", None, "field", None)
    return jax.shard_map(
        on_device, mesh=mesh, in_specs=in_specs, out_specs=out_specs, check_vma=False
    )
```

time: 315 us -> 85.1 us (0.27)
  blocking collectives: 165 us -> 0 us
  Pallas kernels: 0 us -> 79 us
  other arithmetic: 49.1 us -> 0.76 us
  starting transfers between devices: 45.3 us -> 0 us
  local copies, waits for them, and re-layouts: 47.3 us -> 4.9 us
  waiting for transfers between devices: 6.58 us -> 0 us
    unnamed x1 -> x0, blocking collectives: 104 us -> none
    pallas_call x0 -> x2, Pallas kernels: none -> 79 us  [the longest x1 69.4 us: on_device(): pl.pallas_call(functools.partial(step_kernel, nz, ny, nf), out_shape=jax....]
    all_to_all x1 -> x0, blocking collectives: 60.1 us -> none  [on_device(): lax.all_to_all(outgoing, 'patch', split_axis=0, concat_axis=0, tiled=True)]
    ppermute x14 -> x0, starting transfers between devices: 45.3 us -> none  [the longest x7 31.7 us: extended(): before = lax.ppermute(last, axis, up)]
    scatter-add x1 -> x0, other arithmetic: 44.3 us -> none  [on_device(): divergence.reshape(-1).at[target].add(forces, mode='drop')]
    gather x70 -> x0, local copies, waits for them, and re-layouts: 24.2 us -> none  [the longest x14 4.06 us: side_faces(): north_face = pressure[:, :, :SIDE][link_table[:, 3]]]
    slice x77 -> x0, local copies, waits for them, and re-layouts: 8.68 us -> none  [the longest x12 2.74 us: stencil_values(): jnp.roll(pressure, 1, axis=-1)]
    ppermute x14 -> x0, waiting for transfers between devices: 6.58 us -> none  [the longest x7 6.57 us: extended(): after = lax.ppermute(first, axis, down)]
  transfers between devices with their start and end apart: 14 -> 0, of which waited for: 6 -> 0; matrix products, arithmetic and copies ran while one was open for 25% -> 0% of each run, Pallas kernels for 0% -> 0%
where the time goes in v1:
time: 85.1 us; the launch traced here: 84.7 us
  Pallas kernels  79 us (93%)
  local copies, waits for them, and re-layouts  4.9 us (6%)
    pallas_call x1, Pallas kernels, on_device(): pl.pallas_call(functools.partial(step_kernel, nz, ny, nf), out_shape=jax....  69.4 us
    pallas_call x1, Pallas kernels, on_device(): pl.pallas_call(gradient_kernel, grid=(n_patch // block,), out_shape=jax.S...  9.69 us
    unnamed x8, local copies, waits for them, and re-layouts  3.48 us

profile of v1, /device:TPU:7, one launch (start us, length us, event | category | flops | bytes accessed | tf_op | source)
XLA Modules:
  0.0 84.7 jit_solution(4897825253204204971)
XLA Ops:
  0.0 0.7 select_reduce_fusion
  0.8 0.7 pad.4.tab_ref
  1.4 0.7 tile.4
  2.1 0.1 tile.10
  2.2 0.0 copy-start.1
  2.2 0.9 %copy-done.1 = f32[8,4,1024]{2,1,0:T(4,128)S(1)} copy-done((f32[8,4,1024]{2,1,0:T(4,128)S(1)}, f32[8,4,1024]{2,1,0:T(4,128)}, u32[]{:S(2)}) %copy-start.1) | copy-done | bytes 131096
  3.1 0.0 copy-start.2
  3.1 0.9 %copy-done.2 = f32[8,4,1024]{2,1,0:T(4,128)S(1)} copy-done((f32[8,4,1024]{2,1,0:T(4,128)S(1)}, f32[8,4,1024]{2,1,0:T(4,128)}, u32[]{:S(2)}) %copy-start.2) | copy-done | bytes 131096
  4.0 0.0 copy-start.3
  4.0 0.8 copy-done.3
  4.8 69.4 %step.1.in_ref = bf16[64,7,8,128]{3,2,1,0:T(8,128)(2,1)S(1)} custom-call(s32[64]{0:T(128)S(1)} %broadcast_subtract_fusion.inv_ref, f32[8,4,1024]{2,1,0:T(4,128)S(1)} %copy-done.1, f32[8,4,1024]{2,1,0:T(4,128)S(1)} %copy-done.2, s32[8,128]{1,0:T(8,128)S(1)} %pad.4.tab_ref, f32[1,128]{1,0:T(1,128)S(1)} %compare_select_fusion.frow_ref, s32[64,128]{1,0:T(8,128)S(1)} %bitcast.1), custom_call_target="tpu_custom_call" | custom-call | tf_op jit(solution)/shard_map/step/pallas_call | solution.py:446
  74.1 0.0 copy-start
  74.1 0.9 %copy-done = bf16[64,7,8,128]{3,2,1,0:T(8,128)(2,1)} copy-done((bf16[64,7,8,128]{3,2,1,0:T(8,128)(2,1)}, bf16[64,7,8,128]{3,2,1,0:T(8,128)(2,1)S(1)}, u32[]{:S(2)}) %copy-start) | copy-done | bytes 917528
  75.0 9.7 %gradient.1 = bf16[64,3,4,1024]{3,2,1,0:T(4,128)(2,1)} custom-call(bf16[64,7,8,128]{3,2,1,0:T(8,128)(2,1)} %copy-done), custom_call_target="tpu_custom_call" | custom-call | tf_op jit(solution)/shard_map/gradient/pallas_call | solution.py:493
  (3 shorter events, 0.0 us)
Async XLA Ops:
  2.2 0.9 %copy-start.1 = (f32[8,4,1024]{2,1,0:T(4,128)S(1)}, f32[8,4,1024]{2,1,0:T(4,128)}, u32[]{:S(2)}) copy-start(f32[8,4,1024]{2,1,0:T(4,128)} %p_ref.1) | copy-start | bytes 393220
  3.1 0.9 %copy-start.2 = (f32[8,4,1024]{2,1,0:T(4,128)S(1)}, f32[8,4,1024]{2,1,0:T(4,128)}, u32[]{:S(2)}) copy-start(f32[8,4,1024]{2,1,0:T(4,128)} %d_ref.1) | copy-start | bytes 393220
  4.0 0.8 copy-start.3
  74.1 0.9 %copy-start = (bf16[64,7,8,128]{3,2,1,0:T(8,128)(2,1)}, bf16[64,7,8,128]{3,2,1,0:T(8,128)(2,1)S(1)}, u32[]{:S(2)}) copy-start(bf16[64,7,8,128]{3,2,1,0:T(8,128)(2,1)S(1)} %step.1.in_ref) | copy-start | bytes 2752516

commit v2 on v1

--- a/solution.py
+++ b/solution.py
@@ -68,13 +68,19 @@
     nz,
     ny,
     nf,
-    inv_ref,
+    adv_ref,
+    force_ref,
     p_ref,
     d_ref,
     tab_ref,
+    cell_ref,
+    out_ref,
+    inv_ref,
     frow_ref,
     pc_ref,
-    out_ref,
+    rbuf,
+    turn,
+    stage,
     pa,
     pb,
     src,
@@ -100,7 +106,7 @@
     z_recv,
     a_send,
     a_recv,
-    own_sem,
+    out_sem,
 ):
     patch = lax.axis_index("patch")
     field = lax.axis_index("field")
@@ -130,6 +136,8 @@
         )
         loads.append(pltpu.make_async_copy(d_ref.at[:, x, :], src.at[2, x], load_sem.at[1, x]))
     loads.append(pltpu.make_async_copy(tab_ref, tabs.at[2], load_sem.at[0, PLANES]))
+    cells = pltpu.make_async_copy(cell_ref, pc_ref, load_sem.at[1, PLANES])
+    cells.start()
     for copy in loads:
         copy.start()
 
@@ -140,6 +148,24 @@
     greeted += [along_line(k) for k in (1, -1, 2, -2)]
     for device in greeted:
         pl.semaphore_signal(barrier, inc=1, device_id=device, device_id_type=MESH)
+
+    per_device = force_ref.shape[0]
+    row_lane = lax.broadcasted_iota(jnp.int32, (1, LANES), 1) - per_device * field
+    row = jnp.zeros((1, LANES), jnp.float32)
+    for i in range(per_device):
+        row = jnp.where(row_lane == i, force_ref[i], row)
+    frow_ref[...] = row
+    owners = [adv_ref[i] for i in range(PPD)]
+
+    def find_patch(d, carry):
+        found = jnp.int32(PPD)
+        for i in range(PPD):
+            found = jnp.where(owners[i] == d, jnp.int32(i), found)
+        inv_ref[d] = found
+        return carry
+
+    lax.fori_loop(0, nz * ny, find_patch, 0)
+    cells.wait()
 
     def build_hot(row, carry):
         zrow = lax.div(row, ny)
@@ -357,13 +383,16 @@
 
     lax.fori_loop(0, nz * ny, fill_slot, 0)
 
+    def shift_of(i):
+        a, b = lax.div(i, ny), lax.rem(i, ny)
+        return lax.rem(a + b, nz), b
+
     def remap_copy(i):
-        a, b = lax.div(i, ny), lax.rem(i, ny)
-        dz = lax.rem(a + b, nz)
-        there = lax.rem(z_me + dz, nz) * ny + lax.rem(y_me + b, ny)
+        dz, dy = shift_of(i)
+        there = lax.rem(z_me + dz, nz) * ny + lax.rem(y_me + dy, ny)
         return pltpu.make_async_remote_copy(
             src_ref=sbuf.at[there],
-            dst_ref=out_ref.at[patch],
+            dst_ref=rbuf.at[patch],
             send_sem=a_send.at[i],
             recv_sem=a_recv.at[i],
             device_id=(there, field),
@@ -374,33 +403,23 @@
         remap_copy(i).start()
         return carry
 
-    def wait_copy(i, carry):
-        remap_copy(i).wait()
-        return carry
-
-    own = pltpu.make_async_copy(sbuf.at[patch], out_ref.at[patch], own_sem)
-    own.start()
     lax.fori_loop(1, nz * ny, start_copy, 0)
-    for copy in x_copies + y_copies + z_copies:
-        copy.wait_send()
-    own.wait()
-    lax.fori_loop(1, nz * ny, wait_copy, 0)
-
-
-def gradient_kernel(in_ref, out_ref, turn):
-    lane = lane_iota()
+
     chunk = lax.broadcasted_iota(jnp.int32, (CHUNKS, LANES), 0)
     z = lane % SIDE
-    face_lane = jnp.where(z == 0, SIDE, 2 * SIDE) + chunk * 4 + lane // SIDE
+    spread_lane = jnp.where(z == 0, SIDE, 2 * SIDE) + chunk * 4 + lane // SIDE
     low_corner = (chunk == 0) & (lane < SIDE)
     high_corner = (chunk == CHUNKS - 1) & (lane >= LANES - SIDE)
 
-    def body(s, carry):
-        rows = [in_ref[s, r].astype(jnp.float32) for r in range(PLANES + 3)]
+    def write_out(s):
+        return pltpu.make_async_copy(stage.at[s], out_ref.at[s], out_sem.at[s])
+
+    def form_gradient(ref, s):
+        rows = [ref[s, r].astype(jnp.float32) for r in range(PLANES + 3)]
         for x in range(PLANES):
             center = rows[x + 1]
             face = jnp.broadcast_to(rows[PLANES + 2][x : x + 1, :], (CHUNKS, LANES))
-            face_z = by_lane(face, face_lane)
+            face_z = by_lane(face, spread_lane)
             up = pltpu.roll(center, SIDE, 1)
             down = pltpu.roll(center, LANES - SIDE, 1)
             south = jnp.where(lane < SIDE, pltpu.roll(up, 1, 0), up)
@@ -414,10 +433,33 @@
             turn[2, x] = 0.5 * (above - below)
         for c in range(3):
             for v in range(CHUNKS):
-                out_ref[s, c, :, v * LANES : (v + 1) * LANES] = turn[c, :, v, :].astype(jnp.bfloat16)
-        return carry
-
-    lax.fori_loop(0, in_ref.shape[0], body, 0)
+                stage[s, c, :, v * LANES : (v + 1) * LANES] = turn[c, :, v, :].astype(jnp.bfloat16)
+        write_out(s).start()
+
+    rbuf[patch] = sbuf[patch]
+    form_gradient(rbuf, patch)
+
+    def take_slot(i, carry):
+        remap_copy(i).wait_recv()
+        dz, dy = shift_of(i)
+        origin = lax.rem(z_me + nz - dz, nz) * ny + lax.rem(y_me + ny - dy, ny)
+        form_gradient(rbuf, origin)
+        return carry
+
+    lax.fori_loop(1, nz * ny, take_slot, 0)
+
+    def end_copy(i, carry):
+        remap_copy(i).wait_send()
+        return carry
+
+    def end_write(s, carry):
+        write_out(s).wait()
+        return carry
+
+    for copy in x_copies + y_copies + z_copies:
+        copy.wait_send()
+    lax.fori_loop(1, nz * ny, end_copy, 0)
+    lax.fori_loop(0, nz * ny, end_write, 0)
 
 
 def on_device(pressure_start, divergence, neighbors, advect_slot, point_cell, point_force):
@@ -425,41 +467,30 @@
     nf = lax.axis_size("field")
     ny = math.isqrt(n_patch)
     nz = n_patch // ny
-    field = lax.axis_index("field")
-    per_device = point_force.shape[0]
-    lane = jnp.arange(LANES, dtype=jnp.int32)
-    spread = jnp.tile(point_force, LANES // per_device)
-    frow = jnp.where(lane // per_device == field, spread, 0.0).reshape(1, LANES)
-    table = jnp.pad(neighbors, ((0, 0), (0, LANES - 6)))
     cells = point_cell.reshape(n_patch, -1)
     if cells.shape[1] < LANES:
         cells = jnp.pad(cells, ((0, 0), (0, LANES - cells.shape[1])), constant_values=-1)
-    owner = jnp.arange(n_patch, dtype=jnp.int32)
-    order = jnp.arange(PPD, dtype=jnp.int32)
-    hit = advect_slot[:, None] == owner[None, :]
-    inverse = PPD - jnp.sum(jnp.where(hit, PPD - order[:, None], 0), axis=0, dtype=jnp.int32)
-
-    anywhere = pl.BlockSpec(memory_space=pl.ANY)
-    vmem = pl.BlockSpec(memory_space=pltpu.VMEM)
+
+    far = pl.BlockSpec(memory_space=pltpu.HBM)
+    smem = pl.BlockSpec(memory_space=pltpu.SMEM)
     dma = pltpu.SemaphoreType.DMA
     slot = (PLANES + 3, CHUNKS, LANES)
-    received = pl.pallas_call(
+    return pl.pallas_call(
         functools.partial(step_kernel, nz, ny, nf),
-        out_shape=jax.ShapeDtypeStruct((n_patch,) + slot, jnp.bfloat16),
-        in_specs=[
-            pl.BlockSpec(memory_space=pltpu.SMEM),
-            anywhere,
-            anywhere,
-            anywhere,
-            vmem,
-            vmem,
-        ],
-        out_specs=anywhere,
+        out_shape=jax.ShapeDtypeStruct((n_patch, 3, PLANES, AREA), jnp.bfloat16),
+        in_specs=[smem, smem, far, far, far, far],
+        out_specs=far,
         scratch_shapes=[
+            pltpu.SMEM((n_patch,), jnp.int32),
+            pltpu.VMEM((1, LANES), jnp.float32),
+            pltpu.VMEM((n_patch, LANES), jnp.int32),
+            pltpu.VMEM((n_patch,) + slot, jnp.bfloat16),
+            pltpu.VMEM((3, PLANES, CHUNKS, LANES), jnp.float32),
+            pltpu.VMEM((n_patch, 3, PLANES, AREA), jnp.bfloat16),
             pltpu.VMEM((SLABS, PLANES + 2, PPD, AREA), jnp.float32),
             pltpu.VMEM((SLABS, PLANES + 2, PPD, AREA), jnp.float32),
             pltpu.VMEM((SLABS, PLANES, PPD, AREA), jnp.float32),
-            pltpu.VMEM((SLABS, PPD, LANES), jnp.int32),
+            pltpu.VMEM((SLABS, PPD, 6), jnp.int32),
             pltpu.VMEM((nf, 1, LANES), jnp.float32),
             pltpu.VMEM((ny, 1, LANES), jnp.float32),
             pltpu.VMEM((nz, ny, 1, LANES), jnp.float32),
@@ -481,24 +512,13 @@
             dma((nz - 1,)),
             dma((n_patch,)),
             dma((n_patch,)),
-            dma,
+            dma((n_patch,)),
         ],
         compiler_params=pltpu.CompilerParams(
-            collective_id=0, has_side_effects=True, vmem_limit_bytes=48 * 1024 * 1024
+            collective_id=0, has_side_effects=True, vmem_limit_bytes=67043328
         ),
         name="step",
-    )(inverse, pressure_start, divergence, table, frow, cells)
-
-    block = 8 if n_patch % 8 == 0 else n_patch
-    return pl.pallas_call(
-        gradient_kernel,
-        grid=(n_patch // block,),
-        out_shape=jax.ShapeDtypeStruct((n_patch, 3, PLANES, AREA), jnp.bfloat16),
-        in_specs=[pl.BlockSpec((block,) + slot, lambda i: (i, 0, 0, 0))],
-        out_specs=pl.BlockSpec((block, 3, PLANES, AREA), lambda i: (i, 0, 0, 0)),
-        scratch_shapes=[pltpu.VMEM((3, PLANES, CHUNKS, LANES), jnp.float32)],
-        name="gradient",
-    )(received)
+    )(advect_slot, point_force, pressure_start, divergence, neighbors, cells)
 
 
 def solution(mesh):

time: 85.1 us -> 74.6 us (0.88)
  Pallas kernels: 79 us -> 70.7 us
  local copies, waits for them, and re-layouts: 4.9 us -> 3.09 us
    pallas_call x1 -> x0, Pallas kernels: 9.69 us -> none  [on_device(): pl.pallas_call(gradient_kernel, grid=(n_patch // block,), out_shape=jax.S...]
    pallas_call x1, Pallas kernels: 69.4 us -> 70.7 us  [on_device(): pl.pallas_call(functools.partial(step_kernel, nz, ny, nf), out_shape=jax....]
    unnamed x8 -> x1, local copies, waits for them, and re-layouts: 3.48 us -> 3.09 us
where the time goes in v2:
time: 74.6 us; the launch traced here: 73.8 us
  Pallas kernels  70.7 us (95%)
  local copies, waits for them, and re-layouts  3.09 us (4%)
    pallas_call x1, Pallas kernels, on_device(): pl.pallas_call(functools.partial(step_kernel, nz, ny, nf), out_shape=jax....  70.7 us
    unnamed x1, local copies, waits for them, and re-layouts  3.09 us

profile of v2, /device:TPU:7, one launch (start us, length us, event | category | flops | bytes accessed | tf_op | source)
XLA Modules:
  0.0 73.8 jit_solution(5657287956675039577)
XLA Ops:
  0.0 70.7 %step.1 = bf16[64,3,4,1024]{3,2,1,0:T(4,128)(2,1)} custom-call(s32[8]{0:T(128)} %adv_ref.1, f32[16]{0:T(128)} %force_ref.1, f32[8,4,1024]{2,1,0:T(4,128)} %p_ref.1, f32[8,4,1024]{2,1,0:T(4,128)} %d_ref.1, s32[8,6]{1,0:T(8,128)} %tab_ref.1, s32[64,128]{1,0:T(8,128)} %bitcast.1), custom_call_target="tpu_custom_call" | custom-call | tf_op jit(solution)/shard_map/step/pallas_call | solution.py:478
  70.7 3.1 %copy.8 = bf16[64,3,4,1024]{3,2,1,0:T(4,128)(2,1)} copy(bf16[64,3,4,1024]{3,2,1,0:T(4,128)(2,1)} %step.1) | data formatting | bytes 3145728

commit v3 on v2

--- a/solution.py
+++ b/solution.py
@@ -80,7 +80,8 @@
     pc_ref,
     rbuf,
     turn,
-    stage,
+    adv_smem,
+    force_smem,
     pa,
     pb,
     src,
@@ -136,6 +137,12 @@
         )
         loads.append(pltpu.make_async_copy(d_ref.at[:, x, :], src.at[2, x], load_sem.at[1, x]))
     loads.append(pltpu.make_async_copy(tab_ref, tabs.at[2], load_sem.at[0, PLANES]))
+    small = [
+        pltpu.make_async_copy(force_ref, force_smem, out_sem.at[0]),
+        pltpu.make_async_copy(adv_ref, adv_smem, out_sem.at[1]),
+    ]
+    for copy in small:
+        copy.start()
     cells = pltpu.make_async_copy(cell_ref, pc_ref, load_sem.at[1, PLANES])
     cells.start()
     for copy in loads:
@@ -152,10 +159,12 @@
     per_device = force_ref.shape[0]
     row_lane = lax.broadcasted_iota(jnp.int32, (1, LANES), 1) - per_device * field
     row = jnp.zeros((1, LANES), jnp.float32)
+    for copy in small:
+        copy.wait()
     for i in range(per_device):
-        row = jnp.where(row_lane == i, force_ref[i], row)
+        row = jnp.where(row_lane == i, force_smem[i], row)
     frow_ref[...] = row
-    owners = [adv_ref[i] for i in range(PPD)]
+    owners = [adv_smem[i] for i in range(PPD)]
 
     def find_patch(d, carry):
         found = jnp.int32(PPD)
@@ -164,8 +173,8 @@
         inv_ref[d] = found
         return carry
 
-    lax.fori_loop(0, nz * ny, find_patch, 0)
-    cells.wait()
+
+    base_rows = lax.broadcasted_iota(jnp.int32, (16, LANES), 0).astype(jnp.float32).astype(jnp.bfloat16)
 
     def build_hot(row, carry):
         zrow = lax.div(row, ny)
@@ -181,16 +190,22 @@
         m = jnp.where((e >= 0) & (e < REGION), m, -1)
         n = lax.rem(cell_in_plane, 256)
         lanes = pl.ds(pl.multiple_of(yrow * LANES, LANES), LANES)
-        rows = lax.broadcasted_iota(jnp.int32, (ROWS_HOT, LANES), 0)
-        hot_a[zrow, :, lanes] = jnp.where(rows == m, 1.0, 0.0).astype(jnp.bfloat16)
-        columns = lax.broadcasted_iota(jnp.int32, (256, LANES), 0)
-        hot_b[zrow, :, lanes] = jnp.where(columns == n, 1.0, 0.0).astype(jnp.bfloat16)
+        def one_hot(place, size):
+            at = jnp.clip(place, -1, 256).astype(jnp.float32)
+            at = jnp.broadcast_to(at, (16, LANES)).astype(jnp.bfloat16)
+            one = jnp.ones((16, LANES), jnp.bfloat16)
+            return [
+                jnp.where(base_rows + jnp.bfloat16(16 * b) == at, one, one - one)
+                for b in range(size // 16)
+            ]
+
+        for part in range(ROWS_HOT // 256):
+            for b, block in enumerate(one_hot(m - 256 * part, 256)):
+                hot_a[zrow, part * 256 + b * 16 : part * 256 + (b + 1) * 16, lanes] = block
+        for b, block in enumerate(one_hot(n, 256)):
+            hot_b[zrow, b * 16 : (b + 1) * 16, lanes] = block
         return carry
 
-    half = nz * ny // 2
-    lax.fori_loop(0, half, build_hot, 0)
-    for copy in loads:
-        copy.wait()
     pl.semaphore_wait(barrier, len(greeted))
 
     def send(source, target, s_sem, r_sem, device):
@@ -209,6 +224,8 @@
         send(frow_ref, xbuf.at[field], x_send.at[k - 1], x_recv.at[k - 1], along_x(k))
         for k in range(1, nf)
     ]
+    for copy in loads:
+        copy.wait()
     halo = []
     for i, (k, lo, hi, dlo, dhi) in enumerate(
         ((1, 0, 4, 0, 4), (-1, 0, 4, 0, 4), (2, 1, 4, 2, 4), (-2, 0, 3, 0, 2))
@@ -237,7 +254,9 @@
             send(tabs.at[2], tabs.at[slot], halo_send.at[2, i], halo_recv.at[2, i], there)
         )
 
-    lax.fori_loop(half, nz * ny, build_hot, 0)
+    half = nz * ny // 2
+    cells.wait()
+    lax.fori_loop(0, half, build_hot, 0)
 
     for copy in x_copies:
         copy.wait_recv()
@@ -250,6 +269,8 @@
         for k in range(1, ny)
     ]
     acc[...] = jnp.zeros_like(acc)
+    lax.fori_loop(half, nz * ny, build_hot, 0)
+    lax.fori_loop(0, nz * ny, find_patch, 0)
     for copy in y_copies:
         copy.wait_recv()
     z_copies = [
@@ -259,23 +280,18 @@
     forces[z_me] = ybuf[...]
 
     def add_points(zrow):
-        for part in range(2):
-            for yrow in range(ny):
-                force = forces[zrow, yrow]
-                high = force.astype(jnp.bfloat16)
-                if part == 1:
-                    high = (force - high.astype(jnp.float32)).astype(jnp.bfloat16)
-                wide = jnp.broadcast_to(high.astype(jnp.float32), (16, LANES)).astype(jnp.bfloat16)
-                for b in range(16):
-                    scaled[b * 16 : (b + 1) * 16, yrow * LANES : (yrow + 1) * LANES] = (
-                        hot_b[zrow, b * 16 : (b + 1) * 16, yrow * LANES : (yrow + 1) * LANES] * wide
-                    )
-            acc[...] += lax.dot_general(
-                hot_a[zrow],
-                scaled[...],
-                (((1,), (1,)), ((), ())),
-                preferred_element_type=jnp.float32,
-            )
+        for yrow in range(ny):
+            lanes = slice(yrow * LANES, (yrow + 1) * LANES)
+            wide = jnp.broadcast_to(forces[zrow, yrow], (16, LANES)).astype(jnp.bfloat16)
+            for b in range(16):
+                rows = slice(b * 16, (b + 1) * 16)
+                scaled[rows, lanes] = hot_b[zrow, rows, lanes] * wide
+        acc[...] += lax.dot_general(
+            hot_a[zrow],
+            scaled[...],
+            (((1,), (1,)), ((), ())),
+            preferred_element_type=jnp.float32,
+        )
 
     add_points(z_me)
 
@@ -309,22 +325,28 @@
                 )
 
     def sweep(old, new, lo, hi):
-        def body(g, carry):
+        def relax(g):
             k = lax.div(g, PLANES)
             j = lax.rem(g, PLANES)
             west = chunks_of(old, k, j)
             center = chunks_of(old, k, j + 1)
             east = chunks_of(old, k, j + 2)
             south, north, below, above, _ = side_values(center, idx[k, 2], idx[k, 3], idx[k, 4])
+            result = []
             for v in range(CHUNKS):
                 around = west[v] + east[v] + south[v] + north[v] + below[v] + above[v]
                 source = src[k, j, :, v * LANES : (v + 1) * LANES]
-                new[k, j + 1, :, v * LANES : (v + 1) * LANES] = center[v] + relaxation * (
-                    source - (6.0 * center[v] - around)
-                )
+                result.append(center[v] + relaxation * (source - (6.0 * center[v] - around)))
+            return k, j, result
+
+        def body(i, carry):
+            done = [relax(lo + 2 * i), relax(lo + 2 * i + 1)]
+            for k, j, result in done:
+                for v in range(CHUNKS):
+                    new[k, j + 1, :, v * LANES : (v + 1) * LANES] = result[v]
             return carry
 
-        lax.fori_loop(lo, hi + 1, body, 0)
+        lax.fori_loop(0, (hi + 1 - lo) // 2, body, 0)
 
     fill_ghosts(pa, range(1, SLABS))
     for copy in halo:
@@ -411,9 +433,6 @@
     low_corner = (chunk == 0) & (lane < SIDE)
     high_corner = (chunk == CHUNKS - 1) & (lane >= LANES - SIDE)
 
-    def write_out(s):
-        return pltpu.make_async_copy(stage.at[s], out_ref.at[s], out_sem.at[s])
-
     def form_gradient(ref, s):
         rows = [ref[s, r].astype(jnp.float32) for r in range(PLANES + 3)]
         for x in range(PLANES):
@@ -433,8 +452,7 @@
             turn[2, x] = 0.5 * (above - below)
         for c in range(3):
             for v in range(CHUNKS):
-                stage[s, c, :, v * LANES : (v + 1) * LANES] = turn[c, :, v, :].astype(jnp.bfloat16)
-        write_out(s).start()
+                out_ref[s, c, :, v * LANES : (v + 1) * LANES] = turn[c, :, v, :].astype(jnp.bfloat16)
 
     rbuf[patch] = sbuf[patch]
     form_gradient(rbuf, patch)
@@ -452,14 +470,9 @@
         remap_copy(i).wait_send()
         return carry
 
-    def end_write(s, carry):
-        write_out(s).wait()
-        return carry
-
     for copy in x_copies + y_copies + z_copies:
         copy.wait_send()
     lax.fori_loop(1, nz * ny, end_copy, 0)
-    lax.fori_loop(0, nz * ny, end_write, 0)
 
 
 def on_device(pressure_start, divergence, neighbors, advect_slot, point_cell, point_force):
@@ -472,21 +485,22 @@
         cells = jnp.pad(cells, ((0, 0), (0, LANES - cells.shape[1])), constant_values=-1)
 
     far = pl.BlockSpec(memory_space=pltpu.HBM)
-    smem = pl.BlockSpec(memory_space=pltpu.SMEM)
     dma = pltpu.SemaphoreType.DMA
     slot = (PLANES + 3, CHUNKS, LANES)
+    inputs = (advect_slot, point_force, pressure_start, divergence, neighbors, cells)
     return pl.pallas_call(
         functools.partial(step_kernel, nz, ny, nf),
         out_shape=jax.ShapeDtypeStruct((n_patch, 3, PLANES, AREA), jnp.bfloat16),
-        in_specs=[smem, smem, far, far, far, far],
-        out_specs=far,
+        in_specs=[far, far, far, far, far, far],
+        out_specs=pl.BlockSpec(memory_space=pltpu.VMEM),
         scratch_shapes=[
             pltpu.SMEM((n_patch,), jnp.int32),
             pltpu.VMEM((1, LANES), jnp.float32),
             pltpu.VMEM((n_patch, LANES), jnp.int32),
             pltpu.VMEM((n_patch,) + slot, jnp.bfloat16),
             pltpu.VMEM((3, PLANES, CHUNKS, LANES), jnp.float32),
-            pltpu.VMEM((n_patch, 3, PLANES, AREA), jnp.bfloat16),
+            pltpu.SMEM(advect_slot.shape, jnp.int32),
+            pltpu.SMEM(point_force.shape, jnp.float32),
             pltpu.VMEM((SLABS, PLANES + 2, PPD, AREA), jnp.float32),
             pltpu.VMEM((SLABS, PLANES + 2, PPD, AREA), jnp.float32),
             pltpu.VMEM((SLABS, PLANES, PPD, AREA), jnp.float32),
@@ -512,15 +526,13 @@
             dma((nz - 1,)),
             dma((n_patch,)),
             dma((n_patch,)),
-            dma((n_patch,)),
+            dma((2,)),
         ],
         compiler_params=pltpu.CompilerParams(
-            collective_id=0, has_side_effects=True, vmem_limit_bytes=67043328
+            collective_id=0, has_side_effects=True, vmem_limit_bytes=48*1024*1024
         ),
         name="step",
-    )(advect_slot, point_force, pressure_start, divergence, neighbors, cells)
-
-
+    )(*[pltpu.with_memory_space_constraint(v, pltpu.HBM) for v in inputs])
 def solution(mesh):
     in_specs = (
         P("patch", "field", None),

time: 74.6 us -> 64.9 us (0.87)
  Pallas kernels: 70.7 us -> 62.6 us
  local copies, waits for them, and re-layouts: 3.09 us -> 1.15 us
    pallas_call x1, Pallas kernels: 70.7 us -> 62.6 us  [on_device(): pl.pallas_call(functools.partial(step_kernel, nz, ny, nf), out_shape=jax....]
    unnamed x1, local copies, waits for them, and re-layouts: 3.09 us -> 1.15 us
where the time goes in v3:
time: 64.9 us; the launch traced here: 63.8 us
  Pallas kernels  62.6 us (96%)
  local copies, waits for them, and re-layouts  1.15 us (2%)
    pallas_call x1, Pallas kernels, on_device(): pl.pallas_call(functools.partial(step_kernel, nz, ny, nf), out_shape=jax....  62.6 us

profile of v3, /device:TPU:7, one launch (start us, length us, event | category | flops | bytes accessed | tf_op | source)
XLA Modules:
  0.0 63.8 jit_solution(8213162037724219100)
XLA Ops:
  0.0 62.6 %step.1 = bf16[64,3,4,1024]{3,2,1,0:T(4,128)(2,1)S(1)} custom-call(s32[8]{0:T(128)} %adv_ref.1, f32[16]{0:T(128)} %force_ref.1, f32[8,4,1024]{2,1,0:T(4,128)} %p_ref.1, f32[8,4,1024]{2,1,0:T(4,128)} %d_ref.1, s32[8,6]{1,0:T(8,128)} %tab_ref.1, s32[64,128]{1,0:T(8,128)} %bitcast.1), custom_call_target="tpu_custom_call" | custom-call | tf_op jit(solution)/shard_map/step/pallas_call | solution.py:491
  62.6 1.1 %copy.8 = bf16[64,3,4,1024]{3,2,1,0:T(4,128)(2,1)} copy(bf16[64,3,4,1024]{3,2,1,0:T(4,128)(2,1)S(1)} %step.1) | data formatting | bytes 3145728

commit v4 on v3

--- a/solution.py
+++ b/solution.py
@@ -38,6 +38,9 @@
 def side_values(center, idx_south, idx_north, idx_z):
     lane = lane_iota()
     z = lane % SIDE
+    other_end = jnp.where(
+        z == 0, lane + (SIDE - 1), jnp.where(z == SIDE - 1, lane - (SIDE - 1), lane)
+    )
     up = [pltpu.roll(c, SIDE, 1) for c in center]
     down = [pltpu.roll(c, LANES - SIDE, 1) for c in center]
     first = by_patch(up[CHUNKS - 1], idx_south)
@@ -48,11 +51,7 @@
         north.append(
             jnp.where(lane >= LANES - SIDE, last if v == CHUNKS - 1 else down[v + 1], down[v])
         )
-        swapped = jnp.where(
-            z == 0,
-            pltpu.roll(center[v], LANES - (SIDE - 1), 1),
-            pltpu.roll(center[v], SIDE - 1, 1),
-        )
+        swapped = by_lane(center[v], other_end)
         face = by_patch(swapped, idx_z)
         faces.append(face)
         below.append(jnp.where(z == 0, face, pltpu.roll(center[v], 1, 1)))
@@ -353,7 +352,7 @@
         copy.wait_send()
     sweep(pa, pb, 2, 17)
 
-    for k in range(1, nz):
+    for k in sorted(range(1, nz), key=lambda k: min(k, nz - k)):
         z_copies[k - 1].wait_recv()
         add_points(lax.rem(z_me + (nz - k), nz))
 
@@ -388,15 +387,14 @@
     face_lane = (within % 4) * SIDE + jnp.where(group == 2, SIDE - 1, 0)
     for r in range(PLANES + 2):
         for v in range(CHUNKS):
-            packed[:PPD, r, v, :] = values[r][v] - level
+            packed[:PPD, 2 * r + v // 4, v % 4, :] = values[r][v] - level
     for r in range(1, PLANES + 1):
         south, north, _, _, faces = side_values(values[r], idx[2, 2], idx[2, 3], idx[2, 4])
         row = jnp.where(group == 0, south[0], north[CHUNKS - 1])
         for v in range(CHUNKS):
             use = (chunk_of_lane == v) & ((group == 1) | (group == 2))
             row = jnp.where(use, by_lane(faces[v], face_lane), row)
-        packed[:PPD, PLANES + 2, r - 1, :] = row - level
-        packed[:PPD, PLANES + 2, PLANES + r - 1, :] = jnp.zeros_like(row)
+        packed[:PPD, 2 * PLANES + 4, r - 1, :] = row - level
     packed[PPD] = jnp.zeros_like(packed[PPD])
 
     def fill_slot(d, carry):
@@ -406,8 +404,11 @@
     lax.fori_loop(0, nz * ny, fill_slot, 0)
 
     def shift_of(i):
-        a, b = lax.div(i, ny), lax.rem(i, ny)
-        return lax.rem(a + b, nz), b
+        def far_first(j, size):
+            return size // 2 + (1 - 2 * lax.rem(j, 2)) * lax.div(j + 1, 2)
+
+        a, b = lax.div(i - 1, ny), lax.rem(i - 1, ny)
+        return far_first(lax.rem(a + b + 1, nz), nz), far_first(b, ny)
 
     def remap_copy(i):
         dz, dy = shift_of(i)
@@ -433,11 +434,17 @@
     low_corner = (chunk == 0) & (lane < SIDE)
     high_corner = (chunk == CHUNKS - 1) & (lane >= LANES - SIDE)
 
-    def form_gradient(ref, s):
-        rows = [ref[s, r].astype(jnp.float32) for r in range(PLANES + 3)]
+    def spread_rows(half, s):
+        for r in range(PLANES + 2):
+            for part in range(2):
+                turn[half, r, part * 4 : part * 4 + 4, :] = rbuf[s, 2 * r + part].astype(jnp.float32)
+
+    def form_gradient(half, s):
+        rows = [turn[half, r] for r in range(PLANES + 2)]
+        faces = rbuf[s, 2 * PLANES + 4].astype(jnp.float32)
         for x in range(PLANES):
             center = rows[x + 1]
-            face = jnp.broadcast_to(rows[PLANES + 2][x : x + 1, :], (CHUNKS, LANES))
+            face = jnp.broadcast_to(faces[x : x + 1, :], (CHUNKS, LANES))
             face_z = by_lane(face, spread_lane)
             up = pltpu.roll(center, SIDE, 1)
             down = pltpu.roll(center, LANES - SIDE, 1)
@@ -447,24 +454,31 @@
             north = jnp.where(high_corner, face, north)
             below = jnp.where(z == 0, face_z, pltpu.roll(center, 1, 1))
             above = jnp.where(z == SIDE - 1, face_z, pltpu.roll(center, LANES - 1, 1))
-            turn[0, x] = 0.5 * (rows[x + 2] - rows[x])
-            turn[1, x] = 0.5 * (north - south)
-            turn[2, x] = 0.5 * (above - below)
-        for c in range(3):
-            for v in range(CHUNKS):
-                out_ref[s, c, :, v * LANES : (v + 1) * LANES] = turn[c, :, v, :].astype(jnp.bfloat16)
+            out_ref[s, 0, x] = (0.5 * (rows[x + 2] - rows[x])).astype(jnp.bfloat16)
+            out_ref[s, 1, x] = (0.5 * (north - south)).astype(jnp.bfloat16)
+            out_ref[s, 2, x] = (0.5 * (above - below)).astype(jnp.bfloat16)
+
+    def finish(slots):
+        for half, s in enumerate(slots):
+            spread_rows(half, s)
+        for half, s in enumerate(slots):
+            form_gradient(half, s)
+
+    def origin_of(i):
+        dz, dy = shift_of(i)
+        return lax.rem(z_me + nz - dz, nz) * ny + lax.rem(y_me + ny - dy, ny)
 
     rbuf[patch] = sbuf[patch]
-    form_gradient(rbuf, patch)
-
-    def take_slot(i, carry):
-        remap_copy(i).wait_recv()
-        dz, dy = shift_of(i)
-        origin = lax.rem(z_me + nz - dz, nz) * ny + lax.rem(y_me + ny - dy, ny)
-        form_gradient(rbuf, origin)
+    remap_copy(1).wait_recv()
+    finish([patch, origin_of(1)])
+
+    def take_pair(i, carry):
+        remap_copy(2 * i).wait_recv()
+        remap_copy(2 * i + 1).wait_recv()
+        finish([origin_of(2 * i), origin_of(2 * i + 1)])
         return carry
 
-    lax.fori_loop(1, nz * ny, take_slot, 0)
+    lax.fori_loop(1, nz * ny // 2, take_pair, 0)
 
     def end_copy(i, carry):
         remap_copy(i).wait_send()
@@ -486,11 +500,11 @@
 
     far = pl.BlockSpec(memory_space=pltpu.HBM)
     dma = pltpu.SemaphoreType.DMA
-    slot = (PLANES + 3, CHUNKS, LANES)
+    slot = (2 * PLANES + 5, 4, LANES)
     inputs = (advect_slot, point_force, pressure_start, divergence, neighbors, cells)
     return pl.pallas_call(
         functools.partial(step_kernel, nz, ny, nf),
-        out_shape=jax.ShapeDtypeStruct((n_patch, 3, PLANES, AREA), jnp.bfloat16),
+        out_shape=jax.ShapeDtypeStruct((n_patch, 3, PLANES, CHUNKS, LANES), jnp.bfloat16),
         in_specs=[far, far, far, far, far, far],
         out_specs=pl.BlockSpec(memory_space=pltpu.VMEM),
         scratch_shapes=[
@@ -498,7 +512,7 @@
             pltpu.VMEM((1, LANES), jnp.float32),
             pltpu.VMEM((n_patch, LANES), jnp.int32),
             pltpu.VMEM((n_patch,) + slot, jnp.bfloat16),
-            pltpu.VMEM((3, PLANES, CHUNKS, LANES), jnp.float32),
+            pltpu.VMEM((2, PLANES + 2, CHUNKS, LANES), jnp.float32),
             pltpu.SMEM(advect_slot.shape, jnp.int32),
             pltpu.SMEM(point_force.shape, jnp.float32),
             pltpu.VMEM((SLABS, PLANES + 2, PPD, AREA), jnp.float32),
@@ -532,7 +546,7 @@
             collective_id=0, has_side_effects=True, vmem_limit_bytes=48*1024*1024
         ),
         name="step",
-    )(*[pltpu.with_memory_space_constraint(v, pltpu.HBM) for v in inputs])
+    )(*[pltpu.with_memory_space_constraint(v, pltpu.HBM) for v in inputs]).reshape(n_patch, 3, PLANES, AREA)
 def solution(mesh):
     in_specs = (
         P("patch", "field", None),

time: 64.9 us -> 62.8 us (0.968)
  Pallas kernels: 62.6 us -> 60.3 us
  local copies, waits for them, and re-layouts: 1.15 us -> 1.85 us
    pallas_call x1, Pallas kernels: 62.6 us -> 60.3 us  [on_device(): pl.pallas_call(functools.partial(step_kernel, nz, ny, nf), out_shape=jax....]
    reshape x0 -> x1, local copies, waits for them, and re-layouts: none -> 1.85 us  [on_device(): return pl.pallas_call(functools.partial(step_kernel, nz, ny, nf), out_sha...]
    unnamed x1 -> x0, local copies, waits for them, and re-layouts: 1.15 us -> none
where the time goes in v4:
time: 62.8 us; the launch traced here: 62.2 us
  Pallas kernels  60.3 us (96%)
  local copies, waits for them, and re-layouts  1.85 us (3%)
    pallas_call x1, Pallas kernels, on_device(): pl.pallas_call(functools.partial(step_kernel, nz, ny, nf), out_shape=jax....  60.3 us
    reshape x1, local copies, waits for them, and re-layouts, on_device(): return pl.pallas_call(functools.partial(step_kernel, nz, ny, nf), out_sha...  1.85 us

profile of v4, /device:TPU:7, one launch (start us, length us, event | category | flops | bytes accessed | tf_op | source)
XLA Modules:
  0.0 62.2 jit_solution(13192029755017951989)
XLA Ops:
  0.0 60.3 %step.1 = bf16[64,3,4,8,128]{4,3,2,1,0:T(8,128)(2,1)S(1)} custom-call(s32[8]{0:T(128)} %adv_ref.1, f32[16]{0:T(128)} %force_ref.1, f32[8,4,1024]{2,1,0:T(4,128)} %p_ref.1, f32[8,4,1024]{2,1,0:T(4,128)} %d_ref.1, s32[8,6]{1,0:T(8,128)} %tab_ref.1, s32[64,128]{1,0:T(8,128)} %bitcast.3), custom_call_target="tpu_custom_call" | custom-call | tf_op jit(solution)/shard_map/step/pallas_call | solution.py:505
  60.3 1.9 %reshape.7 = bf16[64,3,4,1024]{3,2,1,0:T(4,128)(2,1)} reshape(bf16[64,3,4,8,128]{4,3,2,1,0:T(8,128)(2,1)S(1)} %step.1) | data formatting | bytes 3145728 | tf_op jit(solution)/shard_map/reshape | solution.py:549

commit v5 on v4

--- a/solution.py
+++ b/solution.py
@@ -35,28 +35,59 @@
     return jnp.take_along_axis(value, index, axis=1, mode="promise_in_bounds")
 
 
-def side_values(center, idx_south, idx_north, idx_z):
+def turned(chunks):
+    group = lane_iota() // SIDE
+    result = []
+    for v in range(CHUNKS):
+        parts = [
+            pltpu.roll(chunks[2 * j + v // 4], SIDE * ((j - v) % 4), 1)
+            if (j - v) % 4
+            else chunks[2 * j + v // 4]
+            for j in range(4)
+        ]
+        low = jnp.where(group == 0, parts[0], parts[1])
+        high = jnp.where(group == 2, parts[2], parts[3])
+        result.append(jnp.where(group < 2, low, high))
+    return result
+
+
+def turned_back(chunks):
+    group = lane_iota() // SIDE
+    result = []
+    for c in range(CHUNKS):
+        j, q = divmod(c, 2)
+        parts = [
+            pltpu.roll(chunks[4 * q + g], SIDE * ((g - j) % 4), 1)
+            if (g - j) % 4
+            else chunks[4 * q + g]
+            for g in range(4)
+        ]
+        low = jnp.where(group == 0, parts[0], parts[1])
+        high = jnp.where(group == 2, parts[2], parts[3])
+        result.append(jnp.where(group < 2, low, high))
+    return result
+
+
+def along_z_values(center, idx_z):
     lane = lane_iota()
     z = lane % SIDE
-    other_end = jnp.where(
-        z == 0, lane + (SIDE - 1), jnp.where(z == SIDE - 1, lane - (SIDE - 1), lane)
-    )
-    up = [pltpu.roll(c, SIDE, 1) for c in center]
-    down = [pltpu.roll(c, LANES - SIDE, 1) for c in center]
-    first = by_patch(up[CHUNKS - 1], idx_south)
-    last = by_patch(down[0], idx_north)
-    south, north, below, above, faces = [], [], [], [], []
-    for v in range(CHUNKS):
-        south.append(jnp.where(lane < SIDE, first if v == 0 else up[v - 1], up[v]))
-        north.append(
-            jnp.where(lane >= LANES - SIDE, last if v == CHUNKS - 1 else down[v + 1], down[v])
-        )
-        swapped = by_lane(center[v], other_end)
-        face = by_patch(swapped, idx_z)
-        faces.append(face)
-        below.append(jnp.where(z == 0, face, pltpu.roll(center[v], 1, 1)))
-        above.append(jnp.where(z == SIDE - 1, face, pltpu.roll(center[v], LANES - 1, 1)))
-    return south, north, below, above, faces
+    lower = jnp.where(z == 0, lane + (SIDE - 1), lane - 1)
+    upper = jnp.where(z == SIDE - 1, lane - (SIDE - 1), lane + 1)
+    below, above = [], []
+    for c in center:
+        mixed = by_patch(c, idx_z)
+        below.append(by_lane(jnp.where(z == SIDE - 1, mixed, c), lower))
+        above.append(by_lane(jnp.where(z == 0, mixed, c), upper))
+    return below, above
+
+
+def along_y_values(center, idx_south, idx_north):
+    lane = lane_iota()
+    up = pltpu.roll(center[CHUNKS - 1], SIDE, 1)
+    down = pltpu.roll(center[0], LANES - SIDE, 1)
+    first = jnp.where(lane < SIDE, by_patch(up, idx_south), up)
+    last = jnp.where(lane >= LANES - SIDE, by_patch(down, idx_north), down)
+    return [first] + center[:-1], center[1:] + [last]
 
 
 def chunks_of(ref, k, row):
@@ -79,6 +110,7 @@
     pc_ref,
     rbuf,
     turn,
+    held,
     adv_smem,
     force_smem,
     pa,
@@ -132,9 +164,9 @@
     loads = []
     for x in range(PLANES):
         loads.append(
-            pltpu.make_async_copy(p_ref.at[:, x, :], pa.at[2, x + 1], load_sem.at[0, x])
+            pltpu.make_async_copy(p_ref.at[:, x, :], held.at[0, x], load_sem.at[0, x])
         )
-        loads.append(pltpu.make_async_copy(d_ref.at[:, x, :], src.at[2, x], load_sem.at[1, x]))
+        loads.append(pltpu.make_async_copy(d_ref.at[:, x, :], held.at[1, x], load_sem.at[1, x]))
     loads.append(pltpu.make_async_copy(tab_ref, tabs.at[2], load_sem.at[0, PLANES]))
     small = [
         pltpu.make_async_copy(force_ref, force_smem, out_sem.at[0]),
@@ -183,7 +215,9 @@
         inside = cell % (x_side * AREA)
         plane = lax.div(q, PPD) * x_side + lax.div(inside, AREA)
         lp = lax.rem(q, PPD)
-        cell_in_plane = lax.rem(inside, AREA)
+        natural = lax.rem(inside, AREA)
+        y = lax.div(natural, SIDE)
+        cell_in_plane = lax.rem(y, CHUNKS) * LANES + lax.div(y, CHUNKS) * SIDE + lax.rem(natural, SIDE)
         e = plane - (line * PLANES - 6)
         m = (lax.div(cell_in_plane, 256) * REGION + e) * PPD + lp
         m = jnp.where((e >= 0) & (e < REGION), m, -1)
@@ -205,6 +239,8 @@
             hot_b[zrow, b * 16 : (b + 1) * 16, lanes] = block
         return carry
 
+    cells.wait()
+    lax.fori_loop(0, nz * ny // 4, build_hot, 0)
     pl.semaphore_wait(barrier, len(greeted))
 
     def send(source, target, s_sem, r_sem, device):
@@ -225,6 +261,15 @@
     ]
     for copy in loads:
         copy.wait()
+    for x in range(PLANES):
+        for kind in range(2):
+            chunks = turned(chunks_of(held, kind, x))
+            for v in range(CHUNKS):
+                lanes = slice(v * LANES, (v + 1) * LANES)
+                if kind == 0:
+                    pa[2, x + 1, :, lanes] = chunks[v]
+                else:
+                    src[2, x, :, lanes] = chunks[v]
     halo = []
     for i, (k, lo, hi, dlo, dhi) in enumerate(
         ((1, 0, 4, 0, 4), (-1, 0, 4, 0, 4), (2, 1, 4, 2, 4), (-2, 0, 3, 0, 2))
@@ -253,9 +298,8 @@
             send(tabs.at[2], tabs.at[slot], halo_send.at[2, i], halo_recv.at[2, i], there)
         )
 
-    half = nz * ny // 2
-    cells.wait()
-    lax.fori_loop(0, half, build_hot, 0)
+    half = nz * ny * 3 // 4
+    lax.fori_loop(nz * ny // 4, half, build_hot, 0)
 
     for copy in x_copies:
         copy.wait_recv()
@@ -307,7 +351,7 @@
         idx[k, 1] = jnp.where(fk == nf - 1, columns[1], own_row)
         idx[k, 2] = columns[2] & (PPD - 1)
         idx[k, 3] = columns[3] & (PPD - 1)
-        idx[k, 4] = jnp.where(z_lane == 0, columns[4], columns[5]) & (PPD - 1)
+        idx[k, 4] = jnp.where(z_lane == 0, columns[5], columns[4]) & (PPD - 1)
 
     def fill_ghosts(ref, edges):
         for k in edges:
@@ -330,7 +374,8 @@
             west = chunks_of(old, k, j)
             center = chunks_of(old, k, j + 1)
             east = chunks_of(old, k, j + 2)
-            south, north, below, above, _ = side_values(center, idx[k, 2], idx[k, 3], idx[k, 4])
+            south, north = along_y_values(center, idx[k, 2], idx[k, 3])
+            below, above = along_z_values(center, idx[k, 4])
             result = []
             for v in range(CHUNKS):
                 around = west[v] + east[v] + south[v] + north[v] + below[v] + above[v]
@@ -373,7 +418,8 @@
     final = refs[SWEEPS % 2]
     fill_ghosts(final, (2, 3))
 
-    values = [chunks_of(final, 2, r) for r in range(PLANES + 2)]
+    ghosts = [chunks_of(final, 2, r) for r in range(PLANES + 2)]
+    values = [turned_back(chunks) for chunks in ghosts]
     level = values[1][0]
     for r in range(1, PLANES + 1):
         for v in range(CHUNKS):
@@ -384,24 +430,24 @@
     group = lane // SIDE
     within = lane % SIDE
     chunk_of_lane = within // 4
+    within_z = lane % SIDE
     face_lane = (within % 4) * SIDE + jnp.where(group == 2, SIDE - 1, 0)
     for r in range(PLANES + 2):
         for v in range(CHUNKS):
             packed[:PPD, 2 * r + v // 4, v % 4, :] = values[r][v] - level
     for r in range(1, PLANES + 1):
-        south, north, _, _, faces = side_values(values[r], idx[2, 2], idx[2, 3], idx[2, 4])
+        south, north = along_y_values(ghosts[r], idx[2, 2], idx[2, 3])
+        below, above = along_z_values(values[r], idx[2, 4])
         row = jnp.where(group == 0, south[0], north[CHUNKS - 1])
         for v in range(CHUNKS):
             use = (chunk_of_lane == v) & ((group == 1) | (group == 2))
-            row = jnp.where(use, by_lane(faces[v], face_lane), row)
+            faces = jnp.where(within_z == 0, below[v], above[v])
+            row = jnp.where(use, by_lane(faces, face_lane), row)
         packed[:PPD, 2 * PLANES + 4, r - 1, :] = row - level
     packed[PPD] = jnp.zeros_like(packed[PPD])
 
-    def fill_slot(d, carry):
+    def fill_slot(d):
         sbuf[d] = packed[inv_ref[d]].astype(jnp.bfloat16)
-        return carry
-
-    lax.fori_loop(0, nz * ny, fill_slot, 0)
 
     def shift_of(i):
         def far_first(j, size):
@@ -410,9 +456,12 @@
         a, b = lax.div(i - 1, ny), lax.rem(i - 1, ny)
         return far_first(lax.rem(a + b + 1, nz), nz), far_first(b, ny)
 
+    def target_of(i):
+        dz, dy = shift_of(i)
+        return lax.rem(z_me + dz, nz) * ny + lax.rem(y_me + dy, ny)
+
     def remap_copy(i):
-        dz, dy = shift_of(i)
-        there = lax.rem(z_me + dz, nz) * ny + lax.rem(y_me + dy, ny)
+        there = target_of(i)
         return pltpu.make_async_remote_copy(
             src_ref=sbuf.at[there],
             dst_ref=rbuf.at[patch],
@@ -422,11 +471,23 @@
             device_id_type=MESH,
         )
 
-    def start_copy(i, carry):
-        remap_copy(i).start()
+    ahead = 3
+
+    def start_copies(i, carry):
+        first = 1 + ahead * i
+        for k in range(ahead):
+            fill_slot(target_of(first + ahead + k))
+        for k in range(ahead):
+            remap_copy(first + k).start()
         return carry
 
-    lax.fori_loop(1, nz * ny, start_copy, 0)
+    rounds = (nz * ny - 1) // ahead
+    for k in range(1, ahead + 1):
+        fill_slot(target_of(k))
+    lax.fori_loop(0, rounds - 1, start_copies, 0)
+    for k in range(nz * ny - ahead, nz * ny):
+        remap_copy(k).start()
+    fill_slot(patch)
 
     chunk = lax.broadcasted_iota(jnp.int32, (CHUNKS, LANES), 0)
     z = lane % SIDE
@@ -513,6 +574,7 @@
             pltpu.VMEM((n_patch, LANES), jnp.int32),
             pltpu.VMEM((n_patch,) + slot, jnp.bfloat16),
             pltpu.VMEM((2, PLANES + 2, CHUNKS, LANES), jnp.float32),
+            pltpu.VMEM((2, PLANES, PPD, AREA), jnp.float32),
             pltpu.SMEM(advect_slot.shape, jnp.int32),
             pltpu.SMEM(point_force.shape, jnp.float32),
             pltpu.VMEM((SLABS, PLANES + 2, PPD, AREA), jnp.float32),

time: 62.8 us -> 62 us (0.987)
    pallas_call x1, Pallas kernels: 60.3 us -> 59.7 us  [on_device(): pl.pallas_call(functools.partial(step_kernel, nz, ny, nf), out_shape=jax....]
where the time goes in v5:
time: 62 us; the launch traced here: 61.5 us
  Pallas kernels  59.7 us (96%)
  local copies, waits for them, and re-layouts  1.85 us (3%)
    pallas_call x1, Pallas kernels, on_device(): pl.pallas_call(functools.partial(step_kernel, nz, ny, nf), out_shape=jax....  59.7 us
    reshape x1, local copies, waits for them, and re-layouts, on_device(): return pl.pallas_call(functools.partial(step_kernel, nz, ny, nf), out_sha...  1.85 us

profile of v5, /device:TPU:7, one launch (start us, length us, event | category | flops | bytes accessed | tf_op | source)
XLA Modules:
  0.0 61.5 jit_solution(6023644932651252850)
XLA Ops:
  0.0 59.7 %step.1 = bf16[64,3,4,8,128]{4,3,2,1,0:T(8,128)(2,1)S(1)} custom-call(s32[8]{0:T(128)} %adv_ref.1, f32[16]{0:T(128)} %force_ref.1, f32[8,4,1024]{2,1,0:T(4,128)} %p_ref.1, f32[8,4,1024]{2,1,0:T(4,128)} %d_ref.1, s32[8,6]{1,0:T(8,128)} %tab_ref.1, s32[64,128]{1,0:T(8,128)} %bitcast.3), custom_call_target="tpu_custom_call" | custom-call | tf_op jit(solution)/shard_map/step/pallas_call | solution.py:566
  59.7 1.9 %reshape.7 = bf16[64,3,4,1024]{3,2,1,0:T(4,128)(2,1)} reshape(bf16[64,3,4,8,128]{4,3,2,1,0:T(8,128)(2,1)S(1)} %step.1) | data formatting | bytes 3145728 | tf_op jit(solution)/shard_map/reshape | solution.py:611

commit v6 on v5

--- a/solution.py
+++ b/solution.py
@@ -454,7 +454,7 @@
             return size // 2 + (1 - 2 * lax.rem(j, 2)) * lax.div(j + 1, 2)
 
         a, b = lax.div(i - 1, ny), lax.rem(i - 1, ny)
-        return far_first(lax.rem(a + b + 1, nz), nz), far_first(b, ny)
+        return far_first(lax.rem(a + 3 * b + 3, nz), nz), far_first(b, ny)
 
     def target_of(i):
         dz, dy = shift_of(i)

time: 62 us -> 61.4 us (level)
  Pallas kernels: 59.7 us -> 59 us
    pallas_call x1, Pallas kernels: 59.7 us -> 59 us  [on_device(): pl.pallas_call(functools.partial(step_kernel, nz, ny, nf), out_shape=jax....]
where the time goes in v6:
time: 61.4 us; the launch traced here: 60.9 us
  Pallas kernels  59 us (96%)
  local copies, waits for them, and re-layouts  1.85 us (3%)
    pallas_call x1, Pallas kernels, on_device(): pl.pallas_call(functools.partial(step_kernel, nz, ny, nf), out_shape=jax....  59 us
    reshape x1, local copies, waits for them, and re-layouts, on_device(): return pl.pallas_call(functools.partial(step_kernel, nz, ny, nf), out_sha...  1.85 us

profile of v6, /device:TPU:7, one launch (start us, length us, event | category | flops | bytes accessed | tf_op | source)
XLA Modules:
  0.0 60.9 jit_solution(91044031393019639)
XLA Ops:
  0.0 59.0 %step.1 = bf16[64,3,4,8,128]{4,3,2,1,0:T(8,128)(2,1)S(1)} custom-call(s32[8]{0:T(128)} %adv_ref.1, f32[16]{0:T(128)} %force_ref.1, f32[8,4,1024]{2,1,0:T(4,128)} %p_ref.1, f32[8,4,1024]{2,1,0:T(4,128)} %d_ref.1, s32[8,6]{1,0:T(8,128)} %tab_ref.1, s32[64,128]{1,0:T(8,128)} %bitcast.3), custom_call_target="tpu_custom_call" | custom-call | tf_op jit(solution)/shard_map/step/pallas_call | solution.py:566
  59.0 1.9 %reshape.7 = bf16[64,3,4,1024]{3,2,1,0:T(4,128)(2,1)} reshape(bf16[64,3,4,8,128]{4,3,2,1,0:T(8,128)(2,1)S(1)} %step.1) | data formatting | bytes 3145728 | tf_op jit(solution)/shard_map/reshape | solution.py:611
